TPU v7x, 1024 devices: a whole 8x8x8 slice. The times are simulated.
1024 devices in a mesh: ctx: 16 (over z, core), head: 8 (over x), band: 8 (over y).
Axes of the slice: x: 8, y: 8, z: 8, core: 2. Of those that a mesh axis runs over, the one named last changes fastest.
Arguments:
- queries: bfloat16 [131072, 1024], P(('band', 'ctx', 'head')), parts along dimension 0, may hold values from -6 to 6
- key_states: bfloat16 [131072, 1024], P(('band', 'ctx', 'head')), parts along dimension 0, may hold values from -6 to 6
- value_states: bfloat16 [131072, 1024], P(('band', 'ctx', 'head')), parts along dimension 0, may hold values from -6 to 6
- grad_output: bfloat16 [131072, 1024], P(('band', 'ctx', 'head')), parts along dimension 0, may hold values from -24 to 24
- block_slot: int32 [2048], P('band'), parts along dimension 0, may hold values from 0 to 255, as said below
- neighbours: int32 [2048, 8], P('band'), parts along dimension 0, may hold values from 0 to 255, as said below
Outputs:
- grad_queries: bfloat16 [131072, 1024], P(('band', 'ctx', 'head')), parts along dimension 0
- grad_keys: bfloat16 [131072, 1024], P(('band', 'ctx', 'head')), parts along dimension 0
- grad_values: bfloat16 [131072, 1024], P(('band', 'ctx', 'head')), parts along dimension 0
There are 8 independent parts, one for each index of `band`. A program takes and returns all parts, laid end to end along the dimension named above; each array names one. Nothing has to cross between parts.
Inputs may be any that keep to these rules, and one draw needn't show every extreme that they name: `block_slot`: a permutation of the 256 slots. `neighbours`: entry 0 of row b is b. The slot of every other entry lies on a ctx index, slot // 16, at most 1 away cyclically from that of b. These entries are distinct where at least 7 such blocks exist, and else repeat.
All inputs are finite; a program needn't handle non-finite values.
Results may differ from a plain program's by a relative error of at most 0.0088.
Values may be sent and summed in bfloat16 or wider, within the bound.
A program may use at most 128 MiB of HBM per device.

v0:
```python
import math

import jax
import jax.numpy as jnp
from jax import lax
from jax.sharding import PartitionSpec as P

HEAD_DIM = 64
BLOCK_TOK = 64
NBR = 8
REACH = 1


def from_behind(value, axis, steps):
    count = lax.axis_size(axis)
    pairs = [(source, (source + steps) % count) for source in range(count)]
    return lax.ppermute(value, axis, pairs)


def body(queries, key_states, value_states, grad_output, block_slot, neighbours):
    query_loc, key_loc, value_loc, grad_loc = (
        lax.all_to_all(queries, "head", split_axis=1, concat_axis=0, tiled=True),
        lax.all_to_all(key_states, "head", split_axis=1, concat_axis=0, tiled=True),
        lax.all_to_all(value_states, "head", split_axis=1, concat_axis=0, tiled=True),
        lax.all_to_all(grad_output, "head", split_axis=1, concat_axis=0, tiled=True),
    )
    row_count, feat_count = query_loc.shape
    block_count = row_count // BLOCK_TOK
    head_count = feat_count // HEAD_DIM
    ctx_size = lax.axis_size("ctx")
    ctx_here = lax.axis_index("ctx")
    slot_count = block_slot.shape[0]
    slot_ids = jnp.arange(slot_count, dtype=jnp.int32)
    matches = (block_slot[None, :] == slot_ids[:, None]).astype(jnp.int32)
    sphere_of = jnp.sum(matches * slot_ids[None, :], axis=1)
    my_slots = ctx_here * block_count + jnp.arange(block_count, dtype=jnp.int32)
    listed = block_slot[neighbours[sphere_of[my_slots]]]
    key_value = jnp.stack((key_loc, value_loc))
    pieces = []
    for offset in range(-REACH, REACH + 1):
        if offset == 0:
            pieces.append(key_value)
        else:
            pieces.append(from_behind(key_value, "ctx", -offset))
    gathered = jnp.concatenate(pieces, axis=1)
    owner_gap = (listed // block_count - ctx_here + ctx_size + REACH) % ctx_size - REACH
    lookup = (owner_gap + REACH) * block_count + listed % block_count
    span_blocks = gathered.shape[1] // BLOCK_TOK
    kv_table = gathered.reshape(2, span_blocks, BLOCK_TOK, feat_count)
    query_blocks = query_loc.reshape(block_count, BLOCK_TOK, head_count, HEAD_DIM)
    grad_blocks = grad_loc.reshape(block_count, BLOCK_TOK, head_count, HEAD_DIM)
    softmax_scale = HEAD_DIM ** (-0.5)
    group = math.gcd(block_count, max(1, 512 // BLOCK_TOK))
    group_count = block_count // group

    def one_group(group_id):
        first = group_id * group
        chosen = lax.dynamic_slice_in_dim(lookup, first, group, 0)
        keyval_now = kv_table[:, chosen].reshape(2, group, NBR * BLOCK_TOK, head_count, HEAD_DIM)
        key_rows = keyval_now[0]
        value_rows = keyval_now[1]
        query_rows = lax.dynamic_slice_in_dim(query_blocks, first, group, 0)
        grad_rows = lax.dynamic_slice_in_dim(grad_blocks, first, group, 0)
        scores = (
            jnp.einsum("gqhd,gkhd->ghqk", query_rows, key_rows, preferred_element_type=jnp.float32)
            * softmax_scale
        )
        row_max = jnp.max(scores, axis=3, keepdims=True)
        weights = jnp.exp(scores - row_max)
        probability = weights / jnp.sum(weights, axis=3, keepdims=True)
        grad_prob = jnp.einsum(
            "gqhd,gkhd->ghqk", grad_rows, value_rows, preferred_element_type=jnp.float32
        )
        row_delta = jnp.sum(probability * grad_prob, axis=3, keepdims=True)
        score_low = (probability * (grad_prob - row_delta)).astype(jnp.bfloat16)
        prob_low = probability.astype(jnp.bfloat16)
        grad_value = jnp.einsum(
            "ghqk,gqhd->gkhd", prob_low, grad_rows, preferred_element_type=jnp.float32
        )
        grad_key = (
            jnp.einsum("ghqk,gqhd->gkhd", score_low, query_rows, preferred_element_type=jnp.float32)
            * softmax_scale
        )
        grad_query = (
            jnp.einsum("ghqk,gkhd->gqhd", score_low, key_rows, preferred_element_type=jnp.float32)
            * softmax_scale
        )
        both = jnp.stack(
            (
                grad_key.reshape(group, NBR, BLOCK_TOK, feat_count),
                grad_value.reshape(group, NBR, BLOCK_TOK, feat_count),
            ),
            axis=2,
        )
        return (
            grad_query.astype(jnp.bfloat16),
            both.reshape(group * NBR, 2 * BLOCK_TOK * feat_count),
        )

    query_parts, contributions = lax.map(one_group, jnp.arange(group_count, dtype=jnp.int32))
    contributions = contributions.reshape(block_count * NBR, 2 * BLOCK_TOK * feat_count)
    selector = (
        lookup.reshape(-1)[None, :] == jnp.arange(span_blocks, dtype=jnp.int32)[:, None]
    ).astype(jnp.float32)
    grad_flat = jnp.dot(
        selector, contributions, precision=lax.Precision.HIGHEST, preferred_element_type=jnp.float32
    )
    returned = grad_flat.reshape(2 * REACH + 1, block_count, 2, BLOCK_TOK, feat_count)
    summed = returned[REACH]
    for offset in range(-REACH, REACH + 1):
        if offset != 0:
            summed = summed + from_behind(returned[offset + REACH], "ctx", offset)
    grad_keyval = summed.astype(jnp.bfloat16)
    key_rows_out = grad_keyval[:, 0].reshape(row_count, feat_count)
    value_rows_out = grad_keyval[:, 1].reshape(row_count, feat_count)
    query_rows_out = query_parts.reshape(row_count, feat_count)
    out_query, out_key, out_value = (
        lax.all_to_all(query_rows_out, "head", split_axis=0, concat_axis=1, tiled=True),
        lax.all_to_all(key_rows_out, "head", split_axis=0, concat_axis=1, tiled=True),
        lax.all_to_all(value_rows_out, "head", split_axis=0, concat_axis=1, tiled=True),
    )
    return (out_query, out_key, out_value)


def solution(mesh):
    in_specs = (
        P(("band", "ctx", "head"), None),
        P(("band", "ctx", "head"), None),
        P(("band", "ctx", "head"), None),
        P(("band", "ctx", "head"), None),
        P("band"),
        P("band", None),
    )
    out_specs = (
        P(("band", "ctx", "head"), None),
        P(("band", "ctx", "head"), None),
        P(("band", "ctx", "head"), None),
    )
    return jax.shard_map(body, mesh=mesh, in_specs=in_specs, out_specs=out_specs, check_vma=False)
```

profile of v0, /device:TPU:112, one launch (start us, length us, event | category | flops | bytes accessed | tf_op | source)
XLA Modules:
  0.0 240.0 jit_solution(16343978357575740735)
XLA Ops:
  2.7 6.9 %all-to-all-start = ((bf16[128,8,128]{2,0,1:T(8,128)(2,1)}), bf16[128,8,128]{2,0,1:T(8,128)(2,1)S(1)}, u32[]{:S(2)}, u32[]{:S(2)}) async-start(bf16[128,8,128]{2,0,1:T(8,128)(2,1)} %copy.101), calls=%async_computation | async-start | bytes 524288 | tf_op jit(solution)/shard_map/all_to_all | solution.py:23
  11.6 9.9 %all-to-all-done = bf16[128,8,128]{2,0,1:T(8,128)(2,1)S(1)} async-done(((bf16[128,8,128]{2,0,1:T(8,128)(2,1)}), bf16[128,8,128]{2,0,1:T(8,128)(2,1)S(1)}, u32[]{:S(2)}, u32[]{:S(2)}) %all-to-all-start) | async-done | bytes 262176 | tf_op jit(solution)/shard_map/all_to_all | solution.py:23
  21.5 3.4 %all-to-all-start.1 = ((bf16[128,8,128]{2,0,1:T(8,128)(2,1)}), bf16[128,8,128]{2,0,1:T(8,128)(2,1)S(1)}, u32[]{:S(2)}, u32[]{:S(2)}) async-start(bf16[128,8,128]{2,0,1:T(8,128)(2,1)} %copy.103), calls=%async_computation.1 | async-start | bytes 524288 | tf_op jit(solution)/shard_map/all_to_all | solution.py:24
  26.7 8.6 %all-to-all-done.1 = bf16[128,8,128]{2,0,1:T(8,128)(2,1)S(1)} async-done(((bf16[128,8,128]{2,0,1:T(8,128)(2,1)}), bf16[128,8,128]{2,0,1:T(8,128)(2,1)S(1)}, u32[]{:S(2)}, u32[]{:S(2)}) %all-to-all-start.1) | async-done | bytes 262176 | tf_op jit(solution)/shard_map/all_to_all | solution.py:24
  35.3 3.4 %all-to-all-start.2 = ((bf16[128,8,128]{0,2,1:T(8,128)(2,1)}), bf16[128,8,128]{0,2,1:T(8,128)(2,1)S(1)}, u32[]{:S(2)}, u32[]{:S(2)}) async-start(bf16[128,8,128]{0,2,1:T(8,128)(2,1)} %bitcast.18), calls=%async_computation.2 | async-start | bytes 524288 | tf_op jit(solution)/shard_map/all_to_all | solution.py:22
  40.4 12.5 %collective-permute-start.1 = (bf16[2,1024,128]{2,1,0:T(8,128)(2,1)S(1)}, bf16[2,1024,128]{2,1,0:T(8,128)(2,1)S(1)}, u32[]{:S(2)}, u32[]{:S(2)}) collective-permute-start(bf16[2,1024,128]{2,1,0:T(8,128)(2,1)S(1)} %pad_maximum_fusion.2), channel_id=1, source_target_pairs={{0,960},{64,0},{128,64},{192,128},{256,192},{320,256},{384,320},{4... | collective-permute-start | bytes 1572872 | tf_op jit(solution)/shard_map/ppermute | solution.py:17
  52.9 6.8 %all-to-all-start.3 = ((bf16[128,8,128]{0,2,1:T(8,128)(2,1)}), bf16[128,8,128]{0,2,1:T(8,128)(2,1)S(1)}, u32[]{:S(2)}, u32[]{:S(2)}) async-start(bf16[128,8,128]{0,2,1:T(8,128)(2,1)} %bitcast.20), calls=%async_computation.3 | async-start | bytes 524288 | tf_op jit(solution)/shard_map/all_to_all | solution.py:25
  59.8 1.3 gather_fusion.3
  62.1 8.1 %all-to-all-done.3 = bf16[128,8,128]{0,2,1:T(8,128)(2,1)S(1)} async-done(((bf16[128,8,128]{0,2,1:T(8,128)(2,1)}), bf16[128,8,128]{0,2,1:T(8,128)(2,1)S(1)}, u32[]{:S(2)}, u32[]{:S(2)}) %all-to-all-start.3) | async-done | bytes 262176 | tf_op jit(solution)/shard_map/all_to_all | solution.py:25
  70.7 2.3 pad_maximum_fusion.1
  73.0 111.8 %while.12 = (s32[]{:T(128)}, bf16[2,8,64,2,64]{2,1,0,4,3:T(8,128)(2,1)}, f32[2,64,16384]{2,1,0:T(8,128)}, s32[2]{0:T(128)S(1)}, s32[16,8]{1,0:T(8,128)S(1)}, /*i...) while((s32[]{:T(128)}, ...), condition=%wide.region_5.6_spmd, body=%wide.region_1.5_spmd.sunk | while | flops 343540416 | bytes 90863504 | solution.py:100
  75.7 2.4 gather_fusion
  78.0 3.6 %copy.133 = bf16[8,8,2,64,128]{3,1,4,0,2:T(8,128)(2,1)} copy(bf16[8,8,2,64,128]{4,3,2,1,0:T(8,128)(2,1)S(1)} %bitcast.125) | data formatting | bytes 4194304 | tf_op jit(solution)/shard_map/while/body/eval_jaxpr/gather | solution.py:59
  81.7 3.9 %fusion.58 = (bf16[1,8,8,64,128]{3,2,4,1,0:T(8,128)(2,1)S(1)}, bf16[1,8,8,64,128]{3,2,4,1,0:T(8,128)(2,1)}) fusion(bf16[2,8,8,64,128]{3,2,4,1,0:T(8,128)(2,1)} %bitcast.124), kind=kLoop, calls=%fused_computation.72.clone.1 | loop fusion | bytes 4194304 | tf_op jit(solution)/shard_map/while/body/eval_jaxpr/slice | solution.py:61
  85.6 3.2 %squeeze.22 = bf16[8,512,2,64]{1,3,2,0:T(8,128)(2,1)S(1)} reshape(bf16[1,8,8,64,128]{3,2,4,1,0:T(8,128)(2,1)} %get-tuple-element.186) | data formatting | bytes 2097152 | tf_op jit(solution)/shard_map/while/body/eval_jaxpr/squeeze | solution.py:60
  88.8 2.1 squeeze.23
  91.6 1.8 multiply_reduce_fusion.3
  94.8 2.0 convolution_bitcast_fusion.2
  98.2 2.4 %reshape.228 = f32[8,8,1,64,128]{3,1,4,0,2:T(8,128)} reshape(f32[8,512,2,64]{1,3,2,0:T(8,128)S(1)} %multiply_bitcast_fusion.2) | data formatting | bytes 4194304 | tf_op jit(solution)/shard_map/while/body/eval_jaxpr/stack;while/body/eval_jaxpr/reshape | solution.py:88
  100.7 4.4 %reshape.227 = f32[8,8,1,64,128]{3,1,4,0,2:T(8,128)} reshape(f32[8,512,2,64]{1,3,2,0:T(8,128)} %convolution_bitcast_fusion.2) | data formatting | bytes 4194304 | tf_op jit(solution)/shard_map/while/body/eval_jaxpr/stack;while/body/eval_jaxpr/reshape | solution.py:88
  105.0 7.5 %pad_maximum_fusion.4 = f32[8,8,2,64,128]{3,1,4,0,2:T(8,128)} fusion(f32[8,8,1,64,128]{3,1,4,0,2:T(8,128)} %reshape.227, f32[8,8,1,64,128]{3,1,4,0,2:T(8,128)} %reshape.228), kind=kLoop, calls=%fused_computation.5.clone.1 | loop fusion | flops 1048576 | bytes 8388608 | tf_op jit(solution)/shard_map/while/body/eval_jaxpr/stack | solution.py:88
  112.6 6.8 %copy.136 = f32[8,8,2,64,128]{4,3,2,1,0:T(8,128)} copy(f32[8,8,2,64,128]{3,1,4,0,2:T(8,128)} %pad_maximum_fusion.4) | data formatting | bytes 8388608 | tf_op jit(solution)/shard_map/while/body/eval_jaxpr/stack | solution.py:88
  119.3 5.0 %broadcast_in_dim.30 = f32[1,64,16384]{2,1,0:T(8,128)} reshape(f32[8,8,2,64,128]{4,3,2,1,0:T(8,128)} %copy.136) | data formatting | bytes 8388608 | tf_op jit(solution)/shard_map/while/body/jit(dynamic_update_index_in_dim)/broadcast_in_dim | solution.py:100
  124.3 4.5 %constant_dynamic-update-slice_fusion.2 = f32[2,64,16384]{2,1,0:T(8,128)} fusion(f32[2,64,16384]{2,1,0:T(8,128)} %get-tuple-element.208, f32[1,64,16384]{2,1,0:T(8,128)} %broadcast_in_dim.30, s32[]{:T(128)S(6)} %copy.142), kind=kLoop, calls=%fused_computation.25.clone.1 | loop fusion | bytes 8388612 | tf_op jit(solution)/shard_map/while/body/jit(dynamic_update_index_in_dim)/dynamic_update_slice | solution.py:100
  131.6 2.4 gather_fusion
  133.9 3.6 %copy.133 = bf16[8,8,2,64,128]{3,1,4,0,2:T(8,128)(2,1)} copy(bf16[8,8,2,64,128]{4,3,2,1,0:T(8,128)(2,1)S(1)} %bitcast.125) | data formatting | bytes 4194304 | tf_op jit(solution)/shard_map/while/body/eval_jaxpr/gather | solution.py:59
  137.6 3.9 %fusion.58 = (bf16[1,8,8,64,128]{3,2,4,1,0:T(8,128)(2,1)S(1)}, bf16[1,8,8,64,128]{3,2,4,1,0:T(8,128)(2,1)}) fusion(bf16[2,8,8,64,128]{3,2,4,1,0:T(8,128)(2,1)} %bitcast.124), kind=kLoop, calls=%fused_computation.72.clone.1 | loop fusion | bytes 4194304 | tf_op jit(solution)/shard_map/while/body/eval_jaxpr/slice | solution.py:61
  141.5 3.2 %squeeze.22 = bf16[8,512,2,64]{1,3,2,0:T(8,128)(2,1)S(1)} reshape(bf16[1,8,8,64,128]{3,2,4,1,0:T(8,128)(2,1)} %get-tuple-element.186) | data formatting | bytes 2097152 | tf_op jit(solution)/shard_map/while/body/eval_jaxpr/squeeze | solution.py:60
  144.7 2.1 squeeze.23
  147.5 1.8 multiply_reduce_fusion.3
  150.7 2.0 convolution_bitcast_fusion.2
  154.1 2.4 %reshape.228 = f32[8,8,1,64,128]{3,1,4,0,2:T(8,128)} reshape(f32[8,512,2,64]{1,3,2,0:T(8,128)S(1)} %multiply_bitcast_fusion.2) | data formatting | bytes 4194304 | tf_op jit(solution)/shard_map/while/body/eval_jaxpr/stack;while/body/eval_jaxpr/reshape | solution.py:88
  156.6 4.4 %reshape.227 = f32[8,8,1,64,128]{3,1,4,0,2:T(8,128)} reshape(f32[8,512,2,64]{1,3,2,0:T(8,128)} %convolution_bitcast_fusion.2) | data formatting | bytes 4194304 | tf_op jit(solution)/shard_map/while/body/eval_jaxpr/stack;while/body/eval_jaxpr/reshape | solution.py:88
  161.0 7.5 %pad_maximum_fusion.4 = f32[8,8,2,64,128]{3,1,4,0,2:T(8,128)} fusion(f32[8,8,1,64,128]{3,1,4,0,2:T(8,128)} %reshape.227, f32[8,8,1,64,128]{3,1,4,0,2:T(8,128)} %reshape.228), kind=kLoop, calls=%fused_computation.5.clone.1 | loop fusion | flops 1048576 | bytes 8388608 | tf_op jit(solution)/shard_map/while/body/eval_jaxpr/stack | solution.py:88
  168.5 6.8 %copy.136 = f32[8,8,2,64,128]{4,3,2,1,0:T(8,128)} copy(f32[8,8,2,64,128]{3,1,4,0,2:T(8,128)} %pad_maximum_fusion.4) | data formatting | bytes 8388608 | tf_op jit(solution)/shard_map/while/body/eval_jaxpr/stack | solution.py:88
  175.3 5.0 %broadcast_in_dim.30 = f32[1,64,16384]{2,1,0:T(8,128)} reshape(f32[8,8,2,64,128]{4,3,2,1,0:T(8,128)} %copy.136) | data formatting | bytes 8388608 | tf_op jit(solution)/shard_map/while/body/jit(dynamic_update_index_in_dim)/broadcast_in_dim | solution.py:100
  180.2 4.6 %constant_dynamic-update-slice_fusion.2 = f32[2,64,16384]{2,1,0:T(8,128)} fusion(f32[2,64,16384]{2,1,0:T(8,128)} %get-tuple-element.208, f32[1,64,16384]{2,1,0:T(8,128)} %broadcast_in_dim.30, s32[]{:T(128)S(6)} %copy.142), kind=kLoop, calls=%fused_computation.25.clone.1 | loop fusion | bytes 8388612 | tf_op jit(solution)/shard_map/while/body/jit(dynamic_update_index_in_dim)/dynamic_update_slice | solution.py:100
  184.8 5.9 %fusion.9 = f32[48,16384]{1,0:T(8,128)S(1)} fusion(f32[128,16384]{1,0:T(8,128)} %bitcast.127, s32[128]{0:T(128)S(1)} %copy-done.11), kind=kOutput, calls=%fused_computation.36 | convolution fusion | flops 1207965696 | bytes 11534848 | tf_op jit(solution)/shard_map/dot_general | solution.py:105
  190.9 1.2 copy.124
  192.1 1.2 copy.125
  193.3 3.0 %collective-permute-start.2 = (f32[16,2,64,128]{3,2,1,0:T(8,128)}, f32[16,2,64,128]{3,2,1,0:T(8,128)S(1)}, u32[]{:S(2)}, u32[]{:S(2)}) collective-permute-start(f32[16,2,64,128]{3,2,1,0:T(8,128)} %bitcast.56), channel_id=1, source_target_pairs={{0,960},{64,0},{128,64},{192,128},{256,192},{320,256},{384,320},{4... | collective-permute-start | bytes 3145736 | tf_op jit(solution)/shard_map/ppermute | solution.py:17
  196.4 1.3 all_to_all.102
  198.4 3.4 %all-to-all-start.4 = ((bf16[8,128,128]{1,2,0:T(8,128)(2,1)}), bf16[8,128,128]{1,2,0:T(8,128)(2,1)S(1)}, u32[]{:S(2)}, u32[]{:S(2)}) async-start(bf16[8,128,128]{1,2,0:T(8,128)(2,1)} %copy.111), calls=%async_computation.4 | async-start | bytes 524288 | tf_op jit(solution)/shard_map/all_to_all | solution.py:118
  202.1 7.0 %collective-permute-done.3 = f32[16,2,64,128]{3,2,1,0:T(8,128)S(1)} collective-permute-done((f32[16,2,64,128]{3,2,1,0:T(8,128)}, f32[16,2,64,128]{3,2,1,0:T(8,128)S(1)}, u32[]{:S(2)}, u32[]{:S(2)}) %collective-permute-start.3) | collective-permute-done | bytes 1048608 | tf_op jit(solution)/shard_map/ppermute | solution.py:17
  210.1 2.1 all-to-all-done.4
  212.2 12.9 %all_to_all.121 = bf16[8,128,128]{2,1,0:T(8,128)(2,1)S(1)} all-to-all(bf16[8,128,128]{2,1,0:T(8,128)(2,1)S(1)} %bitcast.140), channel_id=1, replica_groups=mesh['ctx'=16,'head'=8,'band'=8] {'head'}, dimensions={0} | all-to-all | bytes 524288 | tf_op jit(solution)/shard_map/all_to_all | solution.py:119
  225.1 3.4 %all-to-all-start.6 = ((bf16[8,128,128]{2,1,0:T(8,128)(2,1)}), bf16[8,128,128]{2,1,0:T(8,128)(2,1)S(1)}, u32[]{:S(2)}, u32[]{:S(2)}) async-start(bf16[8,128,128]{2,1,0:T(8,128)(2,1)} %bitcast.28), calls=%async_computation.6 | async-start | bytes 524288 | tf_op jit(solution)/shard_map/all_to_all | solution.py:120
  230.4 8.5 %all-to-all-done.6 = bf16[8,128,128]{2,1,0:T(8,128)(2,1)S(1)} async-done(((bf16[8,128,128]{2,1,0:T(8,128)(2,1)}), bf16[8,128,128]{2,1,0:T(8,128)(2,1)S(1)}, u32[]{:S(2)}, u32[]{:S(2)}) %all-to-all-start.6) | async-done | bytes 262176 | tf_op jit(solution)/shard_map/all_to_all | solution.py:120
  (108 shorter events, 25.3 us)
Async XLA Ops:
  0.6 24.3 %copy-start.10 = (s32[256,8]{0,1:T(8,128)S(1)}, s32[256,8]{0,1:T(8,128)}, u32[]{:S(2)}) copy-start(s32[256,8]{0,1:T(8,128)} %param.13) | copy-start | bytes 24580
  0.6 24.4 %copy-start.8 = (bf16[128,1024]{1,0:T(8,128)(2,1)S(1)}, bf16[128,1024]{1,0:T(8,128)(2,1)}, u32[]{:S(2)}) copy-start(bf16[128,1024]{1,0:T(8,128)(2,1)} %param.8) | copy-start | bytes 786436
  0.7 25.2 %copy-start = (s32[256]{0:T(256)S(1)}, s32[256]{0:T(256)}, u32[]{:S(2)}) copy-start(s32[256]{0:T(256)} %param.12) | copy-start | bytes 3076
  2.7 36.8 %copy-start.9 = (bf16[128,1024]{1,0:T(8,128)(2,1)S(1)}, bf16[128,1024]{1,0:T(8,128)(2,1)}, u32[]{:S(2)}) copy-start(bf16[128,1024]{1,0:T(8,128)(2,1)} %param.11) | copy-start | bytes 786436
  2.7 18.8 %all-to-all-start = ((bf16[128,8,128]{2,0,1:T(8,128)(2,1)}), bf16[128,8,128]{2,0,1:T(8,128)(2,1)S(1)}, u32[]{:S(2)}, u32[]{:S(2)}) async-start(bf16[128,8,128]{2,0,1:T(8,128)(2,1)} %copy.101), calls=%async_computation | async-start | bytes 524288 | tf_op jit(solution)/shard_map/all_to_all | solution.py:23
  21.5 13.8 %all-to-all-start.1 = ((bf16[128,8,128]{2,0,1:T(8,128)(2,1)}), bf16[128,8,128]{2,0,1:T(8,128)(2,1)S(1)}, u32[]{:S(2)}, u32[]{:S(2)}) async-start(bf16[128,8,128]{2,0,1:T(8,128)(2,1)} %copy.103), calls=%async_computation.1 | async-start | bytes 524288 | tf_op jit(solution)/shard_map/all_to_all | solution.py:24
  35.3 17.6 %all-to-all-start.2 = ((bf16[128,8,128]{0,2,1:T(8,128)(2,1)}), bf16[128,8,128]{0,2,1:T(8,128)(2,1)S(1)}, u32[]{:S(2)}, u32[]{:S(2)}) async-start(bf16[128,8,128]{0,2,1:T(8,128)(2,1)} %bitcast.18), calls=%async_computation.2 | async-start | bytes 524288 | tf_op jit(solution)/shard_map/all_to_all | solution.py:22
  40.4 30.2 %collective-permute-start.1 = (bf16[2,1024,128]{2,1,0:T(8,128)(2,1)S(1)}, bf16[2,1024,128]{2,1,0:T(8,128)(2,1)S(1)}, u32[]{:S(2)}, u32[]{:S(2)}) collective-permute-start(bf16[2,1024,128]{2,1,0:T(8,128)(2,1)S(1)} %pad_maximum_fusion.2), channel_id=1, source_target_pairs={{0,960},{64,0},{128,64},{192,128},{256,192},{320,256},{384,320},{4... | collective-permute-start | bytes 1572872 | tf_op jit(solution)/shard_map/ppermute | solution.py:17
  52.9 17.8 %collective-permute-start = (bf16[2,1024,128]{2,1,0:T(8,128)(2,1)S(1)}, bf16[2,1024,128]{2,1,0:T(8,128)(2,1)}, u32[]{:S(2)}, u32[]{:S(2)}) collective-permute-start(bf16[2,1024,128]{2,1,0:T(8,128)(2,1)S(1)} %pad_maximum_fusion.2), channel_id=1, source_target_pairs={{0,64},{64,128},{128,192},{192,256},{256,320},{320,384},{384,448},... | collective-permute-start | bytes 1572872 | tf_op jit(solution)/shard_map/ppermute | solution.py:17
  52.9 17.3 %all-to-all-start.3 = ((bf16[128,8,128]{0,2,1:T(8,128)(2,1)}), bf16[128,8,128]{0,2,1:T(8,128)(2,1)S(1)}, u32[]{:S(2)}, u32[]{:S(2)}) async-start(bf16[128,8,128]{0,2,1:T(8,128)(2,1)} %bitcast.20), calls=%async_computation.3 | async-start | bytes 524288 | tf_op jit(solution)/shard_map/all_to_all | solution.py:25
  73.0 111.8 %copy-start.11 = (s32[128]{0:T(128)S(1)}, s32[128]{0:T(128)}, u32[]{:S(2)}) copy-start(s32[128]{0:T(128)} %fusion.17) | copy-start | bytes 1540
  73.0 1.7 copy-start.2
  73.0 1.7 copy-start.4
  93.8 1.0 copy-start.1
  94.8 2.0 copy-start.6
  96.9 0.8 copy-start.7
  124.3 4.5 %copy-start.3 = (bf16[16,64,2,64]{1,0,3,2:T(8,128)(2,1)S(1)}, bf16[16,64,2,64]{1,0,3,2:T(8,128)(2,1)}, u32[]{:S(2)}) copy-start(bf16[16,64,2,64]{1,0,3,2:T(8,128)(2,1)} %copy-done.2) | copy-start | bytes 786436 | tf_op jit(solution)/shard_map/while
  124.3 4.5 %copy-start.5 = (bf16[16,64,2,64]{1,0,3,2:T(8,128)(2,1)S(1)}, bf16[16,64,2,64]{1,0,3,2:T(8,128)(2,1)}, u32[]{:S(2)}) copy-start(bf16[16,64,2,64]{1,0,3,2:T(8,128)(2,1)} %copy-done.4) | copy-start | bytes 786436 | tf_op jit(solution)/shard_map/while
  128.8 1.8 copy-start.2
  128.8 1.8 copy-start.4
  149.7 1.0 copy-start.1
  150.7 2.0 copy-start.6
  152.9 0.8 copy-start.7
  180.2 4.6 %copy-start.3 = (bf16[16,64,2,64]{1,0,3,2:T(8,128)(2,1)S(1)}, bf16[16,64,2,64]{1,0,3,2:T(8,128)(2,1)}, u32[]{:S(2)}) copy-start(bf16[16,64,2,64]{1,0,3,2:T(8,128)(2,1)} %copy-done.2) | copy-start | bytes 786436 | tf_op jit(solution)/shard_map/while
  180.2 4.6 %copy-start.5 = (bf16[16,64,2,64]{1,0,3,2:T(8,128)(2,1)S(1)}, bf16[16,64,2,64]{1,0,3,2:T(8,128)(2,1)}, u32[]{:S(2)}) copy-start(bf16[16,64,2,64]{1,0,3,2:T(8,128)(2,1)} %copy-done.4) | copy-start | bytes 786436 | tf_op jit(solution)/shard_map/while
  193.3 15.7 %collective-permute-start.3 = (f32[16,2,64,128]{3,2,1,0:T(8,128)}, f32[16,2,64,128]{3,2,1,0:T(8,128)S(1)}, u32[]{:S(2)}, u32[]{:S(2)}) collective-permute-start(f32[16,2,64,128]{3,2,1,0:T(8,128)} %bitcast.59), channel_id=1, source_target_pairs={{0,64},{64,128},{128,192},{192,256},{256,320},{320,384},{384,448},... | collective-permute-start | bytes 3145736 | tf_op jit(solution)/shard_map/ppermute | solution.py:17
  193.3 15.7 %collective-permute-start.2 = (f32[16,2,64,128]{3,2,1,0:T(8,128)}, f32[16,2,64,128]{3,2,1,0:T(8,128)S(1)}, u32[]{:S(2)}, u32[]{:S(2)}) collective-permute-start(f32[16,2,64,128]{3,2,1,0:T(8,128)} %bitcast.56), channel_id=1, source_target_pairs={{0,960},{64,0},{128,64},{192,128},{256,192},{320,256},{384,320},{4... | collective-permute-start | bytes 3145736 | tf_op jit(solution)/shard_map/ppermute | solution.py:17
  198.4 13.8 %all-to-all-start.4 = ((bf16[8,128,128]{1,2,0:T(8,128)(2,1)}), bf16[8,128,128]{1,2,0:T(8,128)(2,1)S(1)}, u32[]{:S(2)}, u32[]{:S(2)}) async-start(bf16[8,128,128]{1,2,0:T(8,128)(2,1)} %copy.111), calls=%async_computation.4 | async-start | bytes 524288 | tf_op jit(solution)/shard_map/all_to_all | solution.py:118
  225.1 13.8 %all-to-all-start.6 = ((bf16[8,128,128]{2,1,0:T(8,128)(2,1)}), bf16[8,128,128]{2,1,0:T(8,128)(2,1)S(1)}, u32[]{:S(2)}, u32[]{:S(2)}) async-start(bf16[8,128,128]{2,1,0:T(8,128)(2,1)} %bitcast.28), calls=%async_computation.6 | async-start | bytes 524288 | tf_op jit(solution)/shard_map/all_to_all | solution.py:120
where the time goes:
time: 244 us; the launch traced here: 240 us
  local copies, waits for them, and re-layouts  101 us (41%)
  waiting for transfers between devices  44.2 us (18%)
  starting transfers between devices  42.9 us (18%)
  other arithmetic  19.3 us (8%)
  matrix products  16.8 us (7%)
  blocking collectives  12.9 us (5%)
    ppermute x4, starting transfers between devices, from_behind(): return lax.ppermute(value, axis, pairs)  15.5 us
    another operation x2, other arithmetic, one_group(): jnp.stack((grad_key.reshape(group, NBR, BLOCK_TOK, feat_count), grad_valu...  15.1 us
    reshape x4, local copies, waits for them, and re-layouts, one_group(): jnp.stack((grad_key.reshape(group, NBR, BLOCK_TOK, feat_count), grad_valu...  13.6 us
    another operation x2, local copies, waits for them, and re-layouts, one_group(): jnp.stack((grad_key.reshape(group, NBR, BLOCK_TOK, feat_count), grad_valu...  13.6 us
    all_to_all x1, blocking collectives, body(): lax.all_to_all(key_rows_out, 'head', split_axis=0, concat_axis=1, tiled=T...  12.9 us
    gather x4, local copies, waits for them, and re-layouts, one_group(): kv_table[:, chosen].reshape(2, group, NBR * BLOCK_TOK, head_count, HEAD_DIM)  12 us
    broadcast_in_dim x2, local copies, waits for them, and re-layouts, body(): lax.map(one_group, jnp.arange(group_count, dtype=jnp.int32))  9.93 us
    all_to_all x1, waiting for transfers between devices, body(): lax.all_to_all(key_states, 'head', split_axis=1, concat_axis=0, tiled=True)  9.9 us
  transfers between devices with their start and end apart: 10, of which 6 were waited for; matrix products, arithmetic and copies ran while one was open for 5% of the time, Pallas kernels for 0%

commit v1 on v0

v1 whole, which is shorter than its diff:
```python
import functools
import math

import jax
import jax.numpy as jnp
from jax import lax
from jax.experimental import pallas as pl
from jax.experimental.pallas import tpu as pltpu
from jax.sharding import PartitionSpec as P

HEAD_DIM = 64
BLOCK_TOK = 64
NBR = 8
MESH = pl.DeviceIdType.MESH
NT = (((1,), (1,)), ((), ()))
NN = (((1,), (0,)), ((), ()))
TN = (((0,), (0,)), ((), ()))


def at_step(step, H):
    return lax.rem(jnp.where(step % 2 == 1, (step + 1) // 2, H - step // 2), H)


def table_kernel(per_ctx, ctx_size, heads, slot_ref, nbr_ref, out_ref, inverse):
    ctx = lax.axis_index("ctx")
    h = lax.axis_index("head")
    per_chunk = per_ctx // heads
    slots = slot_ref.shape[0]
    pairs = per_ctx * NBR
    base = ctx * per_ctx

    def invert(step, carry):
        for k in range(8):
            b = step * 8 + k
            inverse[slot_ref[b]] = b
        return carry

    lax.fori_loop(0, slots // 8, invert, 0)

    def clear(t, carry):
        out_ref[2 * pairs + t] = pairs
        return carry

    lax.fori_loop(0, 3 * per_ctx, clear, 0)

    def one(turn, carry):
        chunk = lax.rem(h + heads - at_step(turn // per_chunk, heads), heads)
        s = chunk * per_chunk + turn % per_chunk
        sphere = inverse[base + s]
        for n in range(NBR):
            slot = slot_ref[nbr_ref[n, sphere]]
            gap = slot // per_ctx - ctx + 1
            gap = jnp.where(gap < 0, gap + ctx_size, gap)
            gap = jnp.where(gap >= ctx_size, gap - ctx_size, gap)
            target = gap * per_ctx + slot % per_ctx
            pair = s * NBR + n
            out_ref[pair] = target
            out_ref[pairs + pair] = out_ref[2 * pairs + target]
            out_ref[2 * pairs + target] = pair
        return carry

    lax.fori_loop(0, per_ctx, one, 0)


def main_kernel(heads, ctx_size, table, q_in, k_in, v_in, g_in, dq_out, dk_out, dv_out,
                q_loc, g_loc, k_span, v_span, run_k, run_v, dq_stage, part_k, part_v, back_k, back_v, sum_k, sum_v,
                in_send, in_recv, fwd_send, fwd_recv, dq_send, dq_recv, ret_send, ret_recv, out_send, out_recv):
    H = heads
    h = lax.axis_index("head")
    c = lax.axis_index("ctx")
    per_chunk = q_in.shape[0]
    T = H * per_chunk
    per_ctx = T
    pairs = per_ctx * NBR
    scale = HEAD_DIM ** -0.5
    ctx_prev = lax.rem(c + ctx_size - 1, ctx_size)
    ctx_next = lax.rem(c + 1, ctx_size)
    ctx_peer = (ctx_prev, ctx_next)

    def peer(d):
        return lax.rem(h + d, H)

    def source(d):
        return lax.rem(h + H - d, H)

    def rows(base, chunk):
        return pl.ds(base + chunk * per_chunk, per_chunk)

    def cols(chunk):
        return pl.ds(pl.multiple_of(chunk * 128, 128), 128)

    barrier = pltpu.get_barrier_semaphore()
    for d in range(1, H):
        pl.semaphore_signal(barrier, inc=1, device_id={"head": peer(d)}, device_id_type=MESH)
    for p in ctx_peer:
        pl.semaphore_signal(barrier, inc=1, device_id={"ctx": p}, device_id_type=MESH)
    pl.semaphore_wait(barrier, H + 1)

    order = [0]
    for step in range(1, H):
        order.append(((step + 1) // 2 if step % 2 else H - step // 2) % H)

    incoming = ((k_in, k_span, T), (v_in, v_span, T), (q_in, q_loc, 0), (g_in, g_loc, 0))

    def in_copy(t, d):
        src, dst, base = incoming[t]
        return pltpu.make_async_remote_copy(
            src_ref=src.at[:, :, cols(peer(d))], dst_ref=dst.at[rows(base, h)],
            send_sem=in_send.at[t, d], recv_sem=in_recv.at[t, d],
            device_id={"head": peer(d)}, device_id_type=MESH)

    def in_own(t):
        src, dst, base = incoming[t]
        return pltpu.make_async_copy(src.at[:, :, cols(h)], dst.at[rows(base, h)], in_recv.at[t, 0])

    def in_wait(t, d):
        src, dst, base = incoming[t]
        pltpu.make_async_remote_copy(
            src_ref=src.at[:, :, cols(peer(d))], dst_ref=dst.at[rows(base, source(d))],
            send_sem=in_send.at[t, d], recv_sem=in_recv.at[t, d],
            device_id={"head": peer(d)}, device_id_type=MESH).wait_recv()

    for t in range(4):
        in_own(t).start()
        for d in order[1:]:
            in_copy(t, d).start()

    def fwd_copy(t, d, way):
        span = incoming[t][1]
        chunk = source(d)
        return pltpu.make_async_remote_copy(
            src_ref=span.at[rows(T, chunk)],
            dst_ref=span.at[rows(2 * T if way == 0 else 0, chunk)],
            send_sem=fwd_send.at[t, d, way], recv_sem=fwd_recv.at[t, d, way],
            device_id={"ctx": ctx_peer[way]}, device_id_type=MESH)

    run_k[pairs] = jnp.zeros(run_k.shape[1:], jnp.float32)
    run_v[pairs] = jnp.zeros(run_v.shape[1:], jnp.float32)

    for t in range(2):
        for d in order:
            if d == 0:
                in_own(t).wait()
            else:
                in_wait(t, d)
            for way in range(2):
                fwd_copy(t, d, way).start()

    def fwd_wait(t, d, way):
        span = incoming[t][1]
        chunk = source(d)
        pltpu.make_async_remote_copy(
            src_ref=span.at[rows(T, chunk)],
            dst_ref=span.at[rows(2 * T if way == 0 else 0, chunk)],
            send_sem=fwd_send.at[t, d, way], recv_sem=fwd_recv.at[t, d, way],
            device_id={"ctx": ctx_peer[way]}, device_id_type=MESH).wait_recv()

    for t in range(2):
        for d in order:
            for way in range(2):
                fwd_wait(t, d, way)

    low = (lax.broadcasted_iota(jnp.int32, (1, 128), 1) < HEAD_DIM).astype(jnp.float32)
    low_mask = low.astype(jnp.bfloat16)
    high_mask = (1.0 - low).astype(jnp.bfloat16)
    low_lanes = lax.broadcasted_iota(jnp.int32, (BLOCK_TOK, 128), 1) < HEAD_DIM
    exp_scale = scale * math.log2(math.e)

    def one_block(s):
        q = q_loc[s]
        g = g_loc[s]
        wq = jnp.concatenate([q * low_mask, q * high_mask], axis=0)
        wg = jnp.concatenate([g * low_mask, g * high_mask], axis=0)
        places = [table[s * NBR + n] for n in range(NBR)]
        ks = jnp.concatenate([k_span[p] for p in places], axis=0)
        vs = jnp.concatenate([v_span[p] for p in places], axis=0)
        scores = lax.dot_general(ks, wq, NT, preferred_element_type=jnp.float32)
        top = jnp.max(scores, axis=0, keepdims=True)
        weights = jnp.exp2((scores - top) * exp_scale)
        inverse = 1.0 / jnp.sum(weights, axis=0, keepdims=True)
        prob = weights * inverse
        grad_prob = lax.dot_general(vs, wg, NT, preferred_element_type=jnp.float32)
        delta = jnp.sum(prob * grad_prob, axis=0, keepdims=True)
        score_low = (prob * (grad_prob - delta)).astype(jnp.bfloat16)
        prob_low = prob.astype(jnp.bfloat16)
        dv = lax.dot_general(prob_low, wg, NN, preferred_element_type=jnp.float32)
        dk = lax.dot_general(score_low, wq, NN, preferred_element_type=jnp.float32)
        dq = lax.dot_general(score_low, ks, TN, preferred_element_type=jnp.float32)
        dq = jnp.where(low_lanes, dq[:BLOCK_TOK], dq[BLOCK_TOK:]) * scale
        dq_stage[s] = dq.astype(jnp.bfloat16)
        for n in range(NBR):
            pair = s * NBR + n
            before = table[pairs + pair]
            part = slice(n * BLOCK_TOK, (n + 1) * BLOCK_TOK)
            run_k[pair] = dk[part] + run_k[before]
            run_v[pair] = dv[part] + run_v[before]

    def dq_copy(d):
        chunk = source(d)
        return pltpu.make_async_remote_copy(
            src_ref=dq_stage.at[rows(0, chunk)], dst_ref=dq_out.at[:, :, cols(h)],
            send_sem=dq_send.at[d], recv_sem=dq_recv.at[d],
            device_id={"head": chunk}, device_id_type=MESH)

    def dq_own():
        return pltpu.make_async_copy(dq_stage.at[rows(0, h)], dq_out.at[:, :, cols(h)], dq_recv.at[0])

    def one_step(step, carry):
        d = at_step(step, H)
        chunk = source(d)

        @pl.when(step == 0)
        def _():
            in_own(2).wait()
            in_own(3).wait()

        @pl.when(step > 0)
        def _():
            in_wait(2, d)
            in_wait(3, d)

        for k in range(per_chunk):
            one_block(chunk * per_chunk + k)

        @pl.when(step == 1)
        def _():
            dq_own().start()

        @pl.when(step > 1)
        def _():
            dq_copy(at_step(step - 1, H)).start()

        return carry

    lax.fori_loop(0, H, one_step, 0)
    dq_copy(order[H - 1]).start()

    last = 2 * pairs
    back_order = order[::-1]

    def ret_copy(d, way, which):
        chunk = peer(d)
        part = (part_k, part_v)[which]
        back = (back_k, back_v)[which]
        return pltpu.make_async_remote_copy(
            src_ref=part.at[rows(way * T, chunk)], dst_ref=back.at[rows(way * T, chunk)],
            send_sem=ret_send.at[which, d, way], recv_sem=ret_recv.at[which, d, way],
            device_id={"ctx": ctx_peer[way]}, device_id_type=MESH)

    for d in back_order:
        chunk = peer(d)
        for way in range(2):
            region = 0 if way == 0 else 2
            for k in range(per_chunk):
                block = chunk * per_chunk + k
                end = table[last + region * per_ctx + block]
                part_k[way * T + block] = (run_k[end] * scale).astype(jnp.bfloat16)
                part_v[way * T + block] = run_v[end].astype(jnp.bfloat16)
        for way in range(2):
            for which in range(2):
                ret_copy(d, way, which).start()

    def out_copy(d, which):
        chunk = peer(d)
        return pltpu.make_async_remote_copy(
            src_ref=(sum_k, sum_v)[which].at[rows(0, chunk)], dst_ref=(dk_out, dv_out)[which].at[:, :, cols(h)],
            send_sem=out_send.at[which, d], recv_sem=out_recv.at[which, d],
            device_id={"head": chunk}, device_id_type=MESH)

    def out_own(which):
        return pltpu.make_async_copy(
            (sum_k, sum_v)[which].at[rows(0, h)], (dk_out, dv_out)[which].at[:, :, cols(h)], out_recv.at[which, 0])

    for d in back_order:
        chunk = peer(d)
        for way in range(2):
            for which in range(2):
                ret_copy(d, way, which).wait_recv()
        for k in range(per_chunk):
            block = chunk * per_chunk + k
            end = table[last + per_ctx + block]
            sum_k[block] = (run_k[end] * scale + back_k[block].astype(jnp.float32)
                            + back_k[T + block].astype(jnp.float32)).astype(jnp.bfloat16)
            sum_v[block] = (run_v[end] + back_v[block].astype(jnp.float32)
                            + back_v[T + block].astype(jnp.float32)).astype(jnp.bfloat16)
        for which in range(2):
            if d == 0:
                out_own(which).start()
            else:
                out_copy(d, which).start()

    dq_own().wait()
    for which in range(2):
        out_own(which).wait()
    for d in order[1:]:
        for t in range(4):
            in_copy(t, d).wait_send()
        dq_copy(d).wait_send()
        pltpu.make_async_remote_copy(
            src_ref=dq_stage.at[rows(0, peer(d))], dst_ref=dq_out.at[:, :, cols(peer(d))],
            send_sem=dq_send.at[d], recv_sem=dq_recv.at[d],
            device_id={"head": peer(d)}, device_id_type=MESH).wait_recv()
        for which in range(2):
            out_copy(d, which).wait_send()
            pltpu.make_async_remote_copy(
                src_ref=(sum_k, sum_v)[which].at[rows(0, source(d))],
                dst_ref=(dk_out, dv_out)[which].at[:, :, cols(source(d))],
                send_sem=out_send.at[which, d], recv_sem=out_recv.at[which, d],
                device_id={"head": source(d)}, device_id_type=MESH).wait_recv()
    for d in order:
        for way in range(2):
            for which in range(2):
                fwd_copy(which, d, way).wait_send()
                ret_copy(d, way, which).wait_send()


def body(queries, key_states, value_states, grad_output, block_slot, neighbours):
    H = lax.axis_size("head")
    C = lax.axis_size("ctx")
    rows, width = queries.shape
    chunk = rows // BLOCK_TOK
    per_ctx = chunk * H
    pairs = per_ctx * NBR
    entries = -(-(2 * pairs + 3 * per_ctx) // 128) * 128
    T = per_ctx
    smem = pl.BlockSpec(memory_space=pltpu.SMEM)
    hbm = pl.BlockSpec(memory_space=pl.ANY)
    table = pl.pallas_call(
        functools.partial(table_kernel, per_ctx, C, H),
        out_shape=jax.ShapeDtypeStruct((entries,), jnp.int32),
        in_specs=[smem, smem],
        out_specs=smem,
        scratch_shapes=[pltpu.SMEM((block_slot.shape[0],), jnp.int32)],
        name="tables",
    )(block_slot, neighbours.T)
    out = jax.ShapeDtypeStruct((chunk, BLOCK_TOK, width), jnp.bfloat16)
    dma = pltpu.SemaphoreType.DMA
    low = jnp.bfloat16
    grads = pl.pallas_call(
        functools.partial(main_kernel, H, C),
        out_shape=(out, out, out),
        in_specs=[smem] + [hbm] * 4,
        out_specs=(hbm, hbm, hbm),
        scratch_shapes=[
            pltpu.VMEM((T, BLOCK_TOK, 128), low), pltpu.VMEM((T, BLOCK_TOK, 128), low),
            pltpu.VMEM((3 * T, BLOCK_TOK, 128), low), pltpu.VMEM((3 * T, BLOCK_TOK, 128), low),
            pltpu.VMEM((pairs + 1, BLOCK_TOK, 128), jnp.float32),
            pltpu.VMEM((pairs + 1, BLOCK_TOK, 128), jnp.float32),
            pltpu.VMEM((T, BLOCK_TOK, 128), low),
            pltpu.VMEM((2 * T, BLOCK_TOK, 128), low), pltpu.VMEM((2 * T, BLOCK_TOK, 128), low),
            pltpu.VMEM((2 * T, BLOCK_TOK, 128), low), pltpu.VMEM((2 * T, BLOCK_TOK, 128), low),
            pltpu.VMEM((T, BLOCK_TOK, 128), low), pltpu.VMEM((T, BLOCK_TOK, 128), low),
            dma((4, H)), dma((4, H)), dma((2, H, 2)), dma((2, H, 2)), dma((H,)), dma((H,)),
            dma((2, H, 2)), dma((2, H, 2)), dma((2, H)), dma((2, H)),
        ],
        compiler_params=pltpu.CompilerParams(collective_id=0, has_side_effects=True, vmem_limit_bytes=56 * 2**20),
        name="attention",
    )(table, *(x.reshape(chunk, BLOCK_TOK, width) for x in (queries, key_states, value_states, grad_output)))
    return tuple(x.reshape(rows, width) for x in grads)


def solution(mesh):
    tokens = P(("band", "ctx", "head"), None)
    in_specs = (tokens, tokens, tokens, tokens, P("band"), P("band", None))
    return jax.shard_map(body, mesh=mesh, in_specs=in_specs, out_specs=(tokens, tokens, tokens), check_vma=False)
```

time: 244 us -> 71.4 us (0.29); the launches traced: 240 us -> 71.1 us
  local copies, waits for them, and re-layouts: 101 us -> 3.46 us
  Pallas kernels: 0 us -> 67 us
  waiting for transfers between devices: 44.2 us -> 0 us
  starting transfers between devices: 42.9 us -> 0 us
  other arithmetic: 19.3 us -> 0 us
  matrix products: 16.8 us -> 0 us
  blocking collectives: 12.9 us -> 0 us
    pallas_call x0 -> x2, Pallas kernels: none -> 67 us  [the longest x1 62.9 us: body(): pl.pallas_call(functools.partial(main_kernel, H, C), out_shape=(out, out,...]
    all_to_all x6 -> x0, waiting for transfers between devices: 37.2 us -> none  [the longest x1 9.9 us: body(): lax.all_to_all(key_states, 'head', split_axis=1, concat_axis=0, tiled=True)]
    all_to_all x6 -> x0, starting transfers between devices: 27.4 us -> none  [the longest x1 6.89 us: body(): lax.all_to_all(key_states, 'head', split_axis=1, concat_axis=0, tiled=True)]
    ppermute x4 -> x0, starting transfers between devices: 15.5 us -> none  [from_behind(): return lax.ppermute(value, axis, pairs)]
    dot_general x9 -> x0, matrix products: 15.3 us -> none  [the longest x1 5.9 us: body(): jnp.dot(selector, contributions, precision=lax.Precision.HIGHEST, preferr...]
    another operation x3 -> x0, other arithmetic: 15.1 us -> none  [the longest x2 15.1 us: one_group(): jnp.stack((grad_key.reshape(group, NBR, BLOCK_TOK, feat_count), grad_valu...]
    gather x9 -> x0, local copies, waits for them, and re-layouts: 14.6 us -> none  [the longest x4 12 us: one_group(): kv_table[:, chosen].reshape(2, group, NBR * BLOCK_TOK, head_count, HEAD_DIM)]
    reshape x6 -> x0, local copies, waits for them, and re-layouts: 14.1 us -> none  [the longest x4 13.6 us: one_group(): jnp.stack((grad_key.reshape(group, NBR, BLOCK_TOK, feat_count), grad_valu...]
  transfers between devices with their start and end apart: 10 -> 0, of which waited for: 6 -> 0; matrix products, arithmetic and copies ran while one was open for 5% -> 0% of each run, Pallas kernels for 0% -> 0%
where the time goes in v1:
time: 71.4 us; the launch traced here: 71.1 us
  Pallas kernels  67 us (94%)
  local copies, waits for them, and re-layouts  3.46 us (5%)
    pallas_call x1, Pallas kernels, body(): pl.pallas_call(functools.partial(main_kernel, H, C), out_shape=(out, out,...  62.9 us
    pallas_call x1, Pallas kernels, body(): pl.pallas_call(functools.partial(table_kernel, per_ctx, C, H), out_shape=...  4.12 us
    unnamed x7, local copies, waits for them, and re-layouts  3.46 us

profile of v1, /device:TPU:112, one launch (start us, length us, event | category | flops | bytes accessed | tf_op | source)
XLA Modules:
  0.0 71.1 jit_solution(7340839868049871370)
XLA Ops:
  0.6 4.1 %tables.1.table = s32[384]{0:T(512)} custom-call(s32[256]{0:T(256)} %slot_ref.1, s32[8,256]{1,0:T(8,128)} %bitcast.15), custom_call_target="tpu_custom_call" | custom-call | tf_op jit(solution)/shard_map/tables/pallas_call | solution.py:328
  4.8 62.9 %attention.1 = (bf16[2,64,1024]{2,1,0:T(8,128)(2,1)}, bf16[2,64,1024]{2,1,0:T(8,128)(2,1)}, bf16[2,64,1024]{2,1,0:T(8,128)(2,1)}) custom-call(s32[384]{0:T(512)} %tables.1.table, bf16[2,64,1024]{2,1,0:T(8,128)(2,1)} %bitcast.11, bf16[2,64,1024]{2,1,0:T(8,128)(2,1)} %bitcast.12, bf16[2,64,1024]{2,1,0:T(8,128)(2,1)} %bitcast.13, bf16[2,64,1024]{2,1,0:T(8,128)(2,1)} %bitcast.14), custom_call_target="tpu_custom_call" | custom-call | tf_op jit(solution)/shard_map/attention/pallas_call | solution.py:339
  67.6 0.0 copy-start.1
  67.6 1.7 %copy.12 = bf16[128,1024]{1,0:T(8,128)(2,1)} copy(bf16[128,1024]{1,0:T(8,128)(2,1)} %bitcast.10) | data formatting | bytes 524288
  69.4 0.0 copy-done.1
  69.4 0.0 copy-start
  69.4 0.7 copy.13
  70.1 0.3 copy-done
  70.4 0.7 copy.14
Async XLA Ops:
  67.6 1.7 %copy-start.1 = (bf16[2,64,1024]{2,1,0:T(8,128)(2,1)S(1)}, bf16[2,64,1024]{2,1,0:T(8,128)(2,1)}, u32[]{:S(2)}) copy-start(bf16[2,64,1024]{2,1,0:T(8,128)(2,1)} %get-tuple-element.7) | copy-start | bytes 786436
  69.4 1.0 %copy-start = (bf16[2,64,1024]{2,1,0:T(8,128)(2,1)S(1)}, bf16[2,64,1024]{2,1,0:T(8,128)(2,1)}, u32[]{:S(2)}) copy-start(bf16[2,64,1024]{2,1,0:T(8,128)(2,1)} %get-tuple-element.8) | copy-start | bytes 786436

commit v2 on v1

--- a/solution.py
+++ b/solution.py
@@ -21,48 +21,17 @@
     return lax.rem(jnp.where(step % 2 == 1, (step + 1) // 2, H - step // 2), H)
 
 
-def table_kernel(per_ctx, ctx_size, heads, slot_ref, nbr_ref, out_ref, inverse):
-    ctx = lax.axis_index("ctx")
-    h = lax.axis_index("head")
-    per_chunk = per_ctx // heads
-    slots = slot_ref.shape[0]
-    pairs = per_ctx * NBR
-    base = ctx * per_ctx
-
-    def invert(step, carry):
-        for k in range(8):
-            b = step * 8 + k
-            inverse[slot_ref[b]] = b
-        return carry
-
-    lax.fori_loop(0, slots // 8, invert, 0)
-
-    def clear(t, carry):
-        out_ref[2 * pairs + t] = pairs
-        return carry
-
-    lax.fori_loop(0, 3 * per_ctx, clear, 0)
-
-    def one(turn, carry):
-        chunk = lax.rem(h + heads - at_step(turn // per_chunk, heads), heads)
-        s = chunk * per_chunk + turn % per_chunk
-        sphere = inverse[base + s]
-        for n in range(NBR):
-            slot = slot_ref[nbr_ref[n, sphere]]
-            gap = slot // per_ctx - ctx + 1
-            gap = jnp.where(gap < 0, gap + ctx_size, gap)
-            gap = jnp.where(gap >= ctx_size, gap - ctx_size, gap)
-            target = gap * per_ctx + slot % per_ctx
-            pair = s * NBR + n
-            out_ref[pair] = target
-            out_ref[pairs + pair] = out_ref[2 * pairs + target]
-            out_ref[2 * pairs + target] = pair
-        return carry
-
-    lax.fori_loop(0, per_ctx, one, 0)
-
-
-def main_kernel(heads, ctx_size, table, q_in, k_in, v_in, g_in, dq_out, dk_out, dv_out,
+def copy_kernel(*refs):
+    half = len(refs) // 2
+    copies = [pltpu.make_async_copy(refs[i], refs[half + i], refs[-1].at[i]) for i in range(half)]
+    for copy in copies:
+        copy.start()
+    for copy in copies:
+        copy.wait()
+
+
+def main_kernel(heads, ctx_size, slot_in, nbr_in, q_in, k_in, v_in, g_in, dq_out, dk_out, dv_out,
+                slot_ref, nbr_ref, table_vec, table, table_sem,
                 q_loc, g_loc, k_span, v_span, run_k, run_v, dq_stage, part_k, part_v, back_k, back_v, sum_k, sum_v,
                 in_send, in_recv, fwd_send, fwd_recv, dq_send, dq_recv, ret_send, ret_recv, out_send, out_recv):
     H = heads
@@ -89,6 +58,10 @@
     def cols(chunk):
         return pl.ds(pl.multiple_of(chunk * 128, 128), 128)
 
+    slot_copy = pltpu.make_async_copy(slot_in, slot_ref, table_sem.at[2])
+    nbr_copy = pltpu.make_async_copy(nbr_in, nbr_ref, table_sem.at[3])
+    slot_copy.start()
+    nbr_copy.start()
     barrier = pltpu.get_barrier_semaphore()
     for d in range(1, H):
         pl.semaphore_signal(barrier, inc=1, device_id={"head": peer(d)}, device_id_type=MESH)
@@ -133,6 +106,46 @@
             dst_ref=span.at[rows(2 * T if way == 0 else 0, chunk)],
             send_sem=fwd_send.at[t, d, way], recv_sem=fwd_recv.at[t, d, way],
             device_id={"ctx": ctx_peer[way]}, device_id_type=MESH)
+
+    slot_copy.wait()
+    nbr_copy.wait()
+    slots = slot_ref.shape[1]
+    slot_row = slot_ref[...]
+    nbr = nbr_ref[...]
+    slot_lane = lax.broadcasted_iota(jnp.int32, (NBR, slots), 1)
+    lane = lax.broadcasted_iota(jnp.int32, (NBR, 128), 1)
+    own = lane * NBR + lax.broadcasted_iota(jnp.int32, (NBR, 128), 0)
+    targets = jnp.zeros((NBR, 128), jnp.int32)
+    for turn in range(per_ctx):
+        s = source(order[turn // per_chunk]) * per_chunk + turn % per_chunk
+        near = jnp.sum(jnp.where(slot_row == c * per_ctx + s, nbr, 0), axis=1, keepdims=True)
+        slot = jnp.sum(jnp.where(slot_lane == near, slot_row, 0), axis=1, keepdims=True)
+        target = jnp.zeros_like(slot)
+        for region, owner in enumerate((ctx_prev, c, ctx_next)):
+            local = slot - owner * per_ctx
+            target = jnp.where((local >= 0) & (local < per_ctx), local + region * per_ctx, target)
+        targets = jnp.where(lane == turn, target, targets)
+    table_vec[0] = targets
+    first_half = pltpu.make_async_copy(table_vec.at[pl.ds(0, 1)], table.at[pl.ds(0, 1)], table_sem.at[0])
+    first_half.start()
+    first_half.wait()
+
+    def chain(turn, carry):
+        before, last = carry
+        for n in range(NBR):
+            target = table[0, n, turn]
+            pair = turn * NBR + n
+            before = jnp.where((targets == target) & (own > pair), pair, before)
+            last = jnp.where(lane == target, pair, last)
+        return before, last
+
+    nothing = jnp.full((NBR, 128), pairs, jnp.int32)
+    before, last = lax.fori_loop(0, per_ctx, chain, (nothing, nothing))
+    table_vec[1] = before
+    table_vec[2] = last
+    second_half = pltpu.make_async_copy(table_vec.at[pl.ds(1, 2)], table.at[pl.ds(1, 2)], table_sem.at[1])
+    second_half.start()
+    second_half.wait()
 
     run_k[pairs] = jnp.zeros(run_k.shape[1:], jnp.float32)
     run_v[pairs] = jnp.zeros(run_v.shape[1:], jnp.float32)
@@ -166,12 +179,12 @@
     low_lanes = lax.broadcasted_iota(jnp.int32, (BLOCK_TOK, 128), 1) < HEAD_DIM
     exp_scale = scale * math.log2(math.e)
 
-    def one_block(s):
+    def one_block(s, turn):
         q = q_loc[s]
         g = g_loc[s]
         wq = jnp.concatenate([q * low_mask, q * high_mask], axis=0)
         wg = jnp.concatenate([g * low_mask, g * high_mask], axis=0)
-        places = [table[s * NBR + n] for n in range(NBR)]
+        places = [table[0, n, turn] for n in range(NBR)]
         ks = jnp.concatenate([k_span[p] for p in places], axis=0)
         vs = jnp.concatenate([v_span[p] for p in places], axis=0)
         scores = lax.dot_general(ks, wq, NT, preferred_element_type=jnp.float32)
@@ -189,8 +202,8 @@
         dq = jnp.where(low_lanes, dq[:BLOCK_TOK], dq[BLOCK_TOK:]) * scale
         dq_stage[s] = dq.astype(jnp.bfloat16)
         for n in range(NBR):
-            pair = s * NBR + n
-            before = table[pairs + pair]
+            pair = turn * NBR + n
+            before = table[1, n, turn]
             part = slice(n * BLOCK_TOK, (n + 1) * BLOCK_TOK)
             run_k[pair] = dk[part] + run_k[before]
             run_v[pair] = dv[part] + run_v[before]
@@ -220,7 +233,7 @@
             in_wait(3, d)
 
         for k in range(per_chunk):
-            one_block(chunk * per_chunk + k)
+            one_block(chunk * per_chunk + k, step * per_chunk + k)
 
         @pl.when(step == 1)
         def _():
@@ -235,7 +248,6 @@
     lax.fori_loop(0, H, one_step, 0)
     dq_copy(order[H - 1]).start()
 
-    last = 2 * pairs
     back_order = order[::-1]
 
     def ret_copy(d, way, which):
@@ -253,7 +265,7 @@
             region = 0 if way == 0 else 2
             for k in range(per_chunk):
                 block = chunk * per_chunk + k
-                end = table[last + region * per_ctx + block]
+                end = table[2, 0, region * per_ctx + block]
                 part_k[way * T + block] = (run_k[end] * scale).astype(jnp.bfloat16)
                 part_v[way * T + block] = run_v[end].astype(jnp.bfloat16)
         for way in range(2):
@@ -278,7 +290,7 @@
                 ret_copy(d, way, which).wait_recv()
         for k in range(per_chunk):
             block = chunk * per_chunk + k
-            end = table[last + per_ctx + block]
+            end = table[2, 0, per_ctx + block]
             sum_k[block] = (run_k[end] * scale + back_k[block].astype(jnp.float32)
                             + back_k[T + block].astype(jnp.float32)).astype(jnp.bfloat16)
             sum_v[block] = (run_v[end] + back_v[block].astype(jnp.float32)
@@ -321,27 +333,20 @@
     chunk = rows // BLOCK_TOK
     per_ctx = chunk * H
     pairs = per_ctx * NBR
-    entries = -(-(2 * pairs + 3 * per_ctx) // 128) * 128
     T = per_ctx
-    smem = pl.BlockSpec(memory_space=pltpu.SMEM)
-    hbm = pl.BlockSpec(memory_space=pl.ANY)
-    table = pl.pallas_call(
-        functools.partial(table_kernel, per_ctx, C, H),
-        out_shape=jax.ShapeDtypeStruct((entries,), jnp.int32),
-        in_specs=[smem, smem],
-        out_specs=smem,
-        scratch_shapes=[pltpu.SMEM((block_slot.shape[0],), jnp.int32)],
-        name="tables",
-    )(block_slot, neighbours.T)
+    hbm = pl.BlockSpec(memory_space=pltpu.HBM)
+    anywhere = pl.BlockSpec(memory_space=pl.ANY)
     out = jax.ShapeDtypeStruct((chunk, BLOCK_TOK, width), jnp.bfloat16)
     dma = pltpu.SemaphoreType.DMA
     low = jnp.bfloat16
     grads = pl.pallas_call(
         functools.partial(main_kernel, H, C),
         out_shape=(out, out, out),
-        in_specs=[smem] + [hbm] * 4,
-        out_specs=(hbm, hbm, hbm),
+        in_specs=[hbm] * 6,
+        out_specs=(anywhere,) * 3,
         scratch_shapes=[
+            pltpu.VMEM((1,) + block_slot.shape, jnp.int32), pltpu.VMEM(neighbours.shape[::-1], jnp.int32),
+            pltpu.VMEM((3, NBR, 128), jnp.int32), pltpu.SMEM((3, NBR, 128), jnp.int32), dma((4,)),
             pltpu.VMEM((T, BLOCK_TOK, 128), low), pltpu.VMEM((T, BLOCK_TOK, 128), low),
             pltpu.VMEM((3 * T, BLOCK_TOK, 128), low), pltpu.VMEM((3 * T, BLOCK_TOK, 128), low),
             pltpu.VMEM((pairs + 1, BLOCK_TOK, 128), jnp.float32),
@@ -353,9 +358,19 @@
             dma((4, H)), dma((4, H)), dma((2, H, 2)), dma((2, H, 2)), dma((H,)), dma((H,)),
             dma((2, H, 2)), dma((2, H, 2)), dma((2, H)), dma((2, H)),
         ],
-        compiler_params=pltpu.CompilerParams(collective_id=0, has_side_effects=True, vmem_limit_bytes=56 * 2**20),
+        compiler_params=pltpu.CompilerParams(collective_id=0, has_side_effects=True, vmem_limit_bytes=24 * 2**20),
         name="attention",
-    )(table, *(x.reshape(chunk, BLOCK_TOK, width) for x in (queries, key_states, value_states, grad_output)))
+    )(*(pltpu.with_memory_space_constraint(x, pltpu.HBM) for x in (block_slot[None], neighbours.T) + tuple(
+        x.reshape(chunk, BLOCK_TOK, width) for x in (queries, key_states, value_states, grad_output))))
+    grads = pl.pallas_call(
+        copy_kernel,
+        out_shape=(out, out, out),
+        in_specs=[anywhere] * 3,
+        out_specs=(anywhere,) * 3,
+        scratch_shapes=[dma((3,))],
+        compiler_params=pltpu.CompilerParams(vmem_limit_bytes=4 * 2**20),
+        name="results",
+    )(*grads)
     return tuple(x.reshape(rows, width) for x in grads)
 
 

time: 71.4 us -> 64.6 us (0.905)
  Pallas kernels: 67 us -> 63 us
  local copies, waits for them, and re-layouts: 3.46 us -> 0 us
    unnamed x7 -> x0, local copies, waits for them, and re-layouts: 3.46 us -> none
    pallas_call x1, Pallas kernels: 4.12 us -> 0.9 us  [body(): pl.pallas_call(copy_kernel, out_shape=(out, out, out), in_specs=[anywhere...]
    pallas_call x1, Pallas kernels: 62.9 us -> 62.1 us  [body(): pl.pallas_call(functools.partial(main_kernel, H, C), out_shape=(out, out,...]
where the time goes in v2:
time: 64.6 us; the launch traced here: 63.6 us
  Pallas kernels  63 us (98%)
    pallas_call x1, Pallas kernels, body(): pl.pallas_call(functools.partial(main_kernel, H, C), out_shape=(out, out,...  62.1 us

profile of v2, /device:TPU:112, one launch (start us, length us, event | category | flops | bytes accessed | tf_op | source)
XLA Modules:
  0.0 63.6 jit_solution(10083411779818232814)
XLA Ops:
  0.6 62.1 %attention.1 = (bf16[2,64,1024]{2,1,0:T(8,128)(2,1)S(1)}, bf16[2,64,1024]{2,1,0:T(8,128)(2,1)S(1)}, bf16[2,64,1024]{2,1,0:T(8,128)(2,1)S(1)}) custom-call(s32[1,256]{1,0:T(1,128)} %bitcast.14, s32[8,256]{1,0:T(8,128)} %bitcast.13, bf16[2,64,1024]{2,1,0:T(8,128)(2,1)} %bitcast.9, bf16[2,64,1024]{2,1,0:T(8,128)(2,1)} %bitcast.10, ...), custom_call_target="tpu_custom_call" | custom-call | tf_op jit(solution)/shard_map/attention/pallas_call | solution.py:342
  62.7 0.9 %results.1 = (bf16[2,64,1024]{2,1,0:T(8,128)(2,1)}, bf16[2,64,1024]{2,1,0:T(8,128)(2,1)}, bf16[2,64,1024]{2,1,0:T(8,128)(2,1)}) custom-call(bf16[2,64,1024]{2,1,0:T(8,128)(2,1)S(1)} %get-tuple-element.9.refs_0_, bf16[2,64,1024]{2,1,0:T(8,128)(2,1)S(1)} %get-tuple-element.10.refs_1_, bf16[2,64,1024]{2,1,0:T(8,128)(2,1)S(1)} %get-tuple-element.11.refs_2_), custom_call_target="tpu_custom_call" | custom-call | tf_op jit(solution)/shard_map/results/pallas_call | solution.py:365

commit v3 on v2

--- a/solution.py
+++ b/solution.py
@@ -11,6 +11,7 @@
 HEAD_DIM = 64
 BLOCK_TOK = 64
 NBR = 8
+TILE_BLOCKS = 2
 MESH = pl.DeviceIdType.MESH
 NT = (((1,), (1,)), ((), ()))
 NN = (((1,), (0,)), ((), ()))
@@ -33,6 +34,7 @@
 def main_kernel(heads, ctx_size, slot_in, nbr_in, q_in, k_in, v_in, g_in, dq_out, dk_out, dv_out,
                 slot_ref, nbr_ref, table_vec, table, table_sem,
                 q_loc, g_loc, k_span, v_span, run_k, run_v, dq_stage, part_k, part_v, back_k, back_v, sum_k, sum_v,
+                score_buf, grad_buf, weight_buf, mixed_buf, top_buf, stat_buf,
                 in_send, in_recv, fwd_send, fwd_recv, dq_send, dq_recv, ret_send, ret_recv, out_send, out_recv):
     H = heads
     h = lax.axis_index("head")
@@ -179,34 +181,97 @@
     low_lanes = lax.broadcasted_iota(jnp.int32, (BLOCK_TOK, 128), 1) < HEAD_DIM
     exp_scale = scale * math.log2(math.e)
 
-    def one_block(s, turn):
-        q = q_loc[s]
-        g = g_loc[s]
-        wq = jnp.concatenate([q * low_mask, q * high_mask], axis=0)
-        wg = jnp.concatenate([g * low_mask, g * high_mask], axis=0)
-        places = [table[0, n, turn] for n in range(NBR)]
-        ks = jnp.concatenate([k_span[p] for p in places], axis=0)
-        vs = jnp.concatenate([v_span[p] for p in places], axis=0)
-        scores = lax.dot_general(ks, wq, NT, preferred_element_type=jnp.float32)
-        top = jnp.max(scores, axis=0, keepdims=True)
-        weights = jnp.exp2((scores - top) * exp_scale)
-        inverse = 1.0 / jnp.sum(weights, axis=0, keepdims=True)
-        prob = weights * inverse
-        grad_prob = lax.dot_general(vs, wg, NT, preferred_element_type=jnp.float32)
-        delta = jnp.sum(prob * grad_prob, axis=0, keepdims=True)
-        score_low = (prob * (grad_prob - delta)).astype(jnp.bfloat16)
-        prob_low = prob.astype(jnp.bfloat16)
-        dv = lax.dot_general(prob_low, wg, NN, preferred_element_type=jnp.float32)
-        dk = lax.dot_general(score_low, wq, NN, preferred_element_type=jnp.float32)
-        dq = lax.dot_general(score_low, ks, TN, preferred_element_type=jnp.float32)
-        dq = jnp.where(low_lanes, dq[:BLOCK_TOK], dq[BLOCK_TOK:]) * scale
-        dq_stage[s] = dq.astype(jnp.bfloat16)
-        for n in range(NBR):
-            pair = turn * NBR + n
-            before = table[1, n, turn]
-            part = slice(n * BLOCK_TOK, (n + 1) * BLOCK_TOK)
-            run_k[pair] = dk[part] + run_k[before]
-            run_v[pair] = dv[part] + run_v[before]
+    tile = TILE_BLOCKS * BLOCK_TOK
+    tiles = NBR // TILE_BLOCKS
+
+    def slot_at(turn):
+        step = turn // per_chunk
+        return source(at_step(step, H)) * per_chunk + turn % per_chunk
+
+    def diagonal(x):
+        return jnp.concatenate([x * low_mask, x * high_mask], axis=0)
+
+    def listed(span, turn, r):
+        return jnp.concatenate([span[table[0, r * TILE_BLOCKS + n, turn]] for n in range(TILE_BLOCKS)], axis=0)
+
+    def fold(x):
+        return x.reshape(tile // 8, 8, 128)
+
+    class Scores:
+        def __init__(self, turn, side):
+            self.turn, self.side = turn, side
+            s = slot_at(turn)
+            self.wq, self.wg = diagonal(q_loc[s]), diagonal(g_loc[s])
+            self.top = None
+
+        def tile(self, r):
+            part = pl.ds(r * tile, tile)
+            scores = lax.dot_general(listed(k_span, self.turn, r), self.wq, NT, preferred_element_type=jnp.float32)
+            score_buf[self.side, part, :] = scores
+            top = jnp.max(fold(scores), axis=0)
+            self.top = top if self.top is None else jnp.maximum(self.top, top)
+            grad_buf[self.side, part, :] = lax.dot_general(
+                listed(v_span, self.turn, r), self.wg, NT, preferred_element_type=jnp.float32)
+
+        def finish(self):
+            top_buf[self.side] = self.top
+
+    class Weights:
+        def __init__(self, turn, side):
+            self.side = side
+            self.top = jnp.max(top_buf[side], axis=0, keepdims=True)
+            self.total = self.mixed = None
+
+        def tile(self, r):
+            part = pl.ds(r * tile, tile)
+            weights = jnp.exp2((score_buf[self.side, part, :] - self.top) * exp_scale)
+            mixed = weights * grad_buf[self.side, part, :]
+            weight_buf[self.side, part, :] = weights
+            mixed_buf[self.side, part, :] = mixed
+            total, mixed = jnp.sum(fold(weights), axis=0), jnp.sum(fold(mixed), axis=0)
+            self.total = total if self.total is None else self.total + total
+            self.mixed = mixed if self.mixed is None else self.mixed + mixed
+
+        def finish(self):
+            inverse = 1.0 / jnp.sum(self.total, axis=0, keepdims=True)
+            stat_buf[self.side, 0:1, :] = inverse
+            stat_buf[self.side, 1:2, :] = jnp.sum(self.mixed, axis=0, keepdims=True) * inverse
+
+    class Gradients:
+        def __init__(self, turn, side):
+            self.turn, self.side = turn, side
+            self.slot = slot_at(turn)
+            self.wq, self.wg = diagonal(q_loc[self.slot]), diagonal(g_loc[self.slot])
+            self.inverse, self.delta = stat_buf[side, 0:1, :], stat_buf[side, 1:2, :]
+            self.dq = None
+
+        def tile(self, r):
+            part = pl.ds(r * tile, tile)
+            prob = weight_buf[self.side, part, :] * self.inverse
+            score_low = (mixed_buf[self.side, part, :] * self.inverse - prob * self.delta).astype(jnp.bfloat16)
+            prob_low = prob.astype(jnp.bfloat16)
+            dv = lax.dot_general(prob_low, self.wg, NN, preferred_element_type=jnp.float32)
+            dk = lax.dot_general(score_low, self.wq, NN, preferred_element_type=jnp.float32)
+            dq = lax.dot_general(score_low, listed(k_span, self.turn, r), TN, preferred_element_type=jnp.float32)
+            self.dq = dq if self.dq is None else self.dq + dq
+            for k in range(TILE_BLOCKS):
+                n = r * TILE_BLOCKS + k
+                pair = self.turn * NBR + n
+                before = table[1, n, self.turn]
+                here = slice(k * BLOCK_TOK, (k + 1) * BLOCK_TOK)
+                run_k[pair] = dk[here] + run_k[before]
+                run_v[pair] = dv[here] + run_v[before]
+
+        def finish(self):
+            dq = jnp.where(low_lanes, self.dq[:BLOCK_TOK], self.dq[BLOCK_TOK:]) * scale
+            dq_stage[self.slot] = dq.astype(jnp.bfloat16)
+
+    def together(*stages):
+        for r in range(tiles):
+            for stage in stages:
+                stage.tile(r)
+        for stage in stages:
+            stage.finish()
 
     def dq_copy(d):
         chunk = source(d)
@@ -218,34 +283,37 @@
     def dq_own():
         return pltpu.make_async_copy(dq_stage.at[rows(0, h)], dq_out.at[:, :, cols(h)], dq_recv.at[0])
 
+    in_own(2).wait()
+    in_own(3).wait()
+    together(Scores(0, 0))
+    together(Weights(0, 0), Scores(1, 1))
+
     def one_step(step, carry):
         d = at_step(step, H)
-        chunk = source(d)
-
-        @pl.when(step == 0)
-        def _():
-            in_own(2).wait()
-            in_own(3).wait()
-
-        @pl.when(step > 0)
-        def _():
-            in_wait(2, d)
-            in_wait(3, d)
-
-        for k in range(per_chunk):
-            one_block(chunk * per_chunk + k, step * per_chunk + k)
-
-        @pl.when(step == 1)
+        in_wait(2, d)
+        in_wait(3, d)
+
+        @pl.when(step == 2)
         def _():
             dq_own().start()
 
-        @pl.when(step > 1)
+        @pl.when(step > 2)
         def _():
-            dq_copy(at_step(step - 1, H)).start()
-
+            dq_copy(at_step(step - 2, H)).start()
+
+        turn = step * per_chunk
+        together(Gradients(turn - 2, 0), Weights(turn - 1, 1), Scores(turn, 0))
+        together(Gradients(turn - 1, 1), Weights(turn, 0), Scores(turn + 1, 1))
         return carry
 
-    lax.fori_loop(0, H, one_step, 0)
+    lax.fori_loop(1, H, one_step, 0)
+    if H == 2:
+        dq_own().start()
+    else:
+        dq_copy(order[H - 2]).start()
+    turn = H * per_chunk
+    together(Gradients(turn - 2, 0), Weights(turn - 1, 1))
+    together(Gradients(turn - 1, 1))
     dq_copy(order[H - 1]).start()
 
     back_order = order[::-1]
@@ -355,6 +423,8 @@
             pltpu.VMEM((2 * T, BLOCK_TOK, 128), low), pltpu.VMEM((2 * T, BLOCK_TOK, 128), low),
             pltpu.VMEM((2 * T, BLOCK_TOK, 128), low), pltpu.VMEM((2 * T, BLOCK_TOK, 128), low),
             pltpu.VMEM((T, BLOCK_TOK, 128), low), pltpu.VMEM((T, BLOCK_TOK, 128), low),
+            *[pltpu.VMEM((2, NBR * BLOCK_TOK, 128), jnp.float32)] * 4,
+            pltpu.VMEM((2, 8, 128), jnp.float32), pltpu.VMEM((2, 8, 128), jnp.float32),
             dma((4, H)), dma((4, H)), dma((2, H, 2)), dma((2, H, 2)), dma((H,)), dma((H,)),
             dma((2, H, 2)), dma((2, H, 2)), dma((2, H)), dma((2, H)),
         ],

time: 64.6 us -> 62.2 us (0.963)
  Pallas kernels: 63 us -> 60.7 us
    pallas_call x1, Pallas kernels: 62.1 us -> 59.8 us  [body(): pl.pallas_call(functools.partial(main_kernel, H, C), out_shape=(out, out,...]
where the time goes in v3:
time: 62.2 us; the launch traced here: 61.4 us
  Pallas kernels  60.7 us (98%)
  between operations  0.64 us (1%)
    pallas_call x1, Pallas kernels, body(): pl.pallas_call(functools.partial(main_kernel, H, C), out_shape=(out, out,...  59.8 us

profile of v3, /device:TPU:112, one launch (start us, length us, event | category | flops | bytes accessed | tf_op | source)
XLA Modules:
  0.0 61.4 jit_solution(355682167191685605)
XLA Ops:
  0.6 59.8 %attention.1 = (bf16[2,64,1024]{2,1,0:T(8,128)(2,1)S(1)}, bf16[2,64,1024]{2,1,0:T(8,128)(2,1)S(1)}, bf16[2,64,1024]{2,1,0:T(8,128)(2,1)S(1)}) custom-call(s32[1,256]{1,0:T(1,128)} %bitcast.14, s32[8,256]{1,0:T(8,128)} %bitcast.13, bf16[2,64,1024]{2,1,0:T(8,128)(2,1)} %bitcast.9, bf16[2,64,1024]{2,1,0:T(8,128)(2,1)} %bitcast.10, ...), custom_call_target="tpu_custom_call" | custom-call | tf_op jit(solution)/shard_map/attention/pallas_call | solution.py:410
  60.4 0.9 %results.1 = (bf16[2,64,1024]{2,1,0:T(8,128)(2,1)}, bf16[2,64,1024]{2,1,0:T(8,128)(2,1)}, bf16[2,64,1024]{2,1,0:T(8,128)(2,1)}) custom-call(bf16[2,64,1024]{2,1,0:T(8,128)(2,1)S(1)} %get-tuple-element.9.refs_0_, bf16[2,64,1024]{2,1,0:T(8,128)(2,1)S(1)} %get-tuple-element.10.refs_1_, bf16[2,64,1024]{2,1,0:T(8,128)(2,1)S(1)} %get-tuple-element.11.refs_2_), custom_call_target="tpu_custom_call" | custom-call | tf_op jit(solution)/shard_map/results/pallas_call | solution.py:435

commit v4 on v3

--- a/solution.py
+++ b/solution.py
@@ -11,7 +11,7 @@
 HEAD_DIM = 64
 BLOCK_TOK = 64
 NBR = 8
-TILE_BLOCKS = 2
+TILE_BLOCKS = 8
 MESH = pl.DeviceIdType.MESH
 NT = (((1,), (1,)), ((), ()))
 NN = (((1,), (0,)), ((), ()))
@@ -24,7 +24,8 @@
 
 def copy_kernel(*refs):
     half = len(refs) // 2
-    copies = [pltpu.make_async_copy(refs[i], refs[half + i], refs[-1].at[i]) for i in range(half)]
+    parts = [(i, k) for i in range(half) for k in range(refs[i].shape[0])]
+    copies = [pltpu.make_async_copy(refs[i].at[k], refs[half + i].at[k], refs[-1].at[i, k]) for i, k in parts]
     for copy in copies:
         copy.start()
     for copy in copies:
@@ -34,7 +35,7 @@
 def main_kernel(heads, ctx_size, slot_in, nbr_in, q_in, k_in, v_in, g_in, dq_out, dk_out, dv_out,
                 slot_ref, nbr_ref, table_vec, table, table_sem,
                 q_loc, g_loc, k_span, v_span, run_k, run_v, dq_stage, part_k, part_v, back_k, back_v, sum_k, sum_v,
-                score_buf, grad_buf, weight_buf, mixed_buf, top_buf, stat_buf,
+                score_buf, weight_buf, mixed_buf, top_buf, total_buf, stat_buf,
                 in_send, in_recv, fwd_send, fwd_recv, dq_send, dq_recv, ret_send, ret_recv, out_send, out_recv):
     H = heads
     h = lax.axis_index("head")
@@ -75,7 +76,7 @@
     for step in range(1, H):
         order.append(((step + 1) // 2 if step % 2 else H - step // 2) % H)
 
-    incoming = ((k_in, k_span, T), (v_in, v_span, T), (q_in, q_loc, 0), (g_in, g_loc, 0))
+    incoming = ((k_in, k_span, T), (q_in, q_loc, 0), (v_in, v_span, T), (g_in, g_loc, 0))
 
     def in_copy(t, d):
         src, dst, base = incoming[t]
@@ -101,7 +102,7 @@
             in_copy(t, d).start()
 
     def fwd_copy(t, d, way):
-        span = incoming[t][1]
+        span = incoming[2 * t][1]
         chunk = source(d)
         return pltpu.make_async_remote_copy(
             src_ref=span.at[rows(T, chunk)],
@@ -152,17 +153,16 @@
     run_k[pairs] = jnp.zeros(run_k.shape[1:], jnp.float32)
     run_v[pairs] = jnp.zeros(run_v.shape[1:], jnp.float32)
 
-    for t in range(2):
-        for d in order:
-            if d == 0:
-                in_own(t).wait()
-            else:
-                in_wait(t, d)
-            for way in range(2):
-                fwd_copy(t, d, way).start()
+    for d in order:
+        if d == 0:
+            in_own(0).wait()
+        else:
+            in_wait(0, d)
+        for way in range(2):
+            fwd_copy(0, d, way).start()
 
     def fwd_wait(t, d, way):
-        span = incoming[t][1]
+        span = incoming[2 * t][1]
         chunk = source(d)
         pltpu.make_async_remote_copy(
             src_ref=span.at[rows(T, chunk)],
@@ -170,10 +170,12 @@
             send_sem=fwd_send.at[t, d, way], recv_sem=fwd_recv.at[t, d, way],
             device_id={"ctx": ctx_peer[way]}, device_id_type=MESH).wait_recv()
 
-    for t in range(2):
+    def span_wait(t):
         for d in order:
             for way in range(2):
                 fwd_wait(t, d, way)
+
+    span_wait(0)
 
     low = (lax.broadcasted_iota(jnp.int32, (1, 128), 1) < HEAD_DIM).astype(jnp.float32)
     low_mask = low.astype(jnp.bfloat16)
@@ -200,8 +202,7 @@
     class Scores:
         def __init__(self, turn, side):
             self.turn, self.side = turn, side
-            s = slot_at(turn)
-            self.wq, self.wg = diagonal(q_loc[s]), diagonal(g_loc[s])
+            self.wq = diagonal(q_loc[slot_at(turn)])
             self.top = None
 
         def tile(self, r):
@@ -210,44 +211,55 @@
             score_buf[self.side, part, :] = scores
             top = jnp.max(fold(scores), axis=0)
             self.top = top if self.top is None else jnp.maximum(self.top, top)
-            grad_buf[self.side, part, :] = lax.dot_general(
-                listed(v_span, self.turn, r), self.wg, NT, preferred_element_type=jnp.float32)
 
         def finish(self):
             top_buf[self.side] = self.top
 
     class Weights:
         def __init__(self, turn, side):
-            self.side = side
+            self.turn, self.side = turn, side
             self.top = jnp.max(top_buf[side], axis=0, keepdims=True)
-            self.total = self.mixed = None
+            self.total = None
 
         def tile(self, r):
             part = pl.ds(r * tile, tile)
             weights = jnp.exp2((score_buf[self.side, part, :] - self.top) * exp_scale)
-            mixed = weights * grad_buf[self.side, part, :]
-            weight_buf[self.side, part, :] = weights
+            weight_buf[self.turn, part, :] = weights
+            total = jnp.sum(fold(weights), axis=0)
+            self.total = total if self.total is None else self.total + total
+
+        def finish(self):
+            total_buf[self.turn] = self.total
+
+    class Mixed:
+        def __init__(self, turn, side):
+            self.turn, self.side = turn, side
+            self.wg = diagonal(g_loc[slot_at(turn)])
+            self.mixed = None
+
+        def tile(self, r):
+            part = pl.ds(r * tile, tile)
+            grad = lax.dot_general(listed(v_span, self.turn, r), self.wg, NT, preferred_element_type=jnp.float32)
+            mixed = weight_buf[self.turn, part, :] * grad
             mixed_buf[self.side, part, :] = mixed
-            total, mixed = jnp.sum(fold(weights), axis=0), jnp.sum(fold(mixed), axis=0)
-            self.total = total if self.total is None else self.total + total
+            mixed = jnp.sum(fold(mixed), axis=0)
             self.mixed = mixed if self.mixed is None else self.mixed + mixed
 
         def finish(self):
-            inverse = 1.0 / jnp.sum(self.total, axis=0, keepdims=True)
-            stat_buf[self.side, 0:1, :] = inverse
-            stat_buf[self.side, 1:2, :] = jnp.sum(self.mixed, axis=0, keepdims=True) * inverse
+            stat_buf[self.side] = self.mixed
 
     class Gradients:
         def __init__(self, turn, side):
             self.turn, self.side = turn, side
             self.slot = slot_at(turn)
             self.wq, self.wg = diagonal(q_loc[self.slot]), diagonal(g_loc[self.slot])
-            self.inverse, self.delta = stat_buf[side, 0:1, :], stat_buf[side, 1:2, :]
+            self.inverse = 1.0 / jnp.sum(total_buf[turn], axis=0, keepdims=True)
+            self.delta = jnp.sum(stat_buf[side], axis=0, keepdims=True) * self.inverse
             self.dq = None
 
         def tile(self, r):
             part = pl.ds(r * tile, tile)
-            prob = weight_buf[self.side, part, :] * self.inverse
+            prob = weight_buf[self.turn, part, :] * self.inverse
             score_low = (mixed_buf[self.side, part, :] * self.inverse - prob * self.delta).astype(jnp.bfloat16)
             prob_low = prob.astype(jnp.bfloat16)
             dv = lax.dot_general(prob_low, self.wg, NN, preferred_element_type=jnp.float32)
@@ -283,15 +295,35 @@
     def dq_own():
         return pltpu.make_async_copy(dq_stage.at[rows(0, h)], dq_out.at[:, :, cols(h)], dq_recv.at[0])
 
+    turns = H * per_chunk
     in_own(2).wait()
-    in_own(3).wait()
+    for way in range(2):
+        fwd_copy(1, 0, way).start()
+    in_own(1).wait()
     together(Scores(0, 0))
     together(Weights(0, 0), Scores(1, 1))
 
-    def one_step(step, carry):
+    def first_step(step, carry):
         d = at_step(step, H)
+        in_wait(1, d)
+        turn = step * per_chunk
+        together(Weights(turn - 1, 1), Scores(turn, 0))
+        together(Weights(turn, 0), Scores(turn + 1, 1))
         in_wait(2, d)
-        in_wait(3, d)
+        for way in range(2):
+            fwd_copy(1, d, way).start()
+        return carry
+
+    lax.fori_loop(1, H, first_step, 0)
+    together(Weights(turns - 1, 1))
+
+    span_wait(1)
+    in_own(3).wait()
+    together(Mixed(0, 0))
+    together(Gradients(0, 0), Mixed(1, 1))
+
+    def second_step(step, carry):
+        in_wait(3, at_step(step, H))
 
         @pl.when(step == 2)
         def _():
@@ -302,18 +334,16 @@
             dq_copy(at_step(step - 2, H)).start()
 
         turn = step * per_chunk
-        together(Gradients(turn - 2, 0), Weights(turn - 1, 1), Scores(turn, 0))
-        together(Gradients(turn - 1, 1), Weights(turn, 0), Scores(turn + 1, 1))
+        together(Gradients(turn - 1, 1), Mixed(turn, 0))
+        together(Gradients(turn, 0), Mixed(turn + 1, 1))
         return carry
 
-    lax.fori_loop(1, H, one_step, 0)
+    lax.fori_loop(1, H, second_step, 0)
     if H == 2:
         dq_own().start()
     else:
         dq_copy(order[H - 2]).start()
-    turn = H * per_chunk
-    together(Gradients(turn - 2, 0), Weights(turn - 1, 1))
-    together(Gradients(turn - 1, 1))
+    together(Gradients(turns - 1, 1))
     dq_copy(order[H - 1]).start()
 
     back_order = order[::-1]
@@ -423,8 +453,9 @@
             pltpu.VMEM((2 * T, BLOCK_TOK, 128), low), pltpu.VMEM((2 * T, BLOCK_TOK, 128), low),
             pltpu.VMEM((2 * T, BLOCK_TOK, 128), low), pltpu.VMEM((2 * T, BLOCK_TOK, 128), low),
             pltpu.VMEM((T, BLOCK_TOK, 128), low), pltpu.VMEM((T, BLOCK_TOK, 128), low),
-            *[pltpu.VMEM((2, NBR * BLOCK_TOK, 128), jnp.float32)] * 4,
-            pltpu.VMEM((2, 8, 128), jnp.float32), pltpu.VMEM((2, 8, 128), jnp.float32),
+            pltpu.VMEM((2, NBR * BLOCK_TOK, 128), jnp.float32), pltpu.VMEM((T, NBR * BLOCK_TOK, 128), jnp.float32),
+            pltpu.VMEM((2, NBR * BLOCK_TOK, 128), jnp.float32),
+            *[pltpu.VMEM((n, 8, 128), jnp.float32) for n in (2, T, 2)],
             dma((4, H)), dma((4, H)), dma((2, H, 2)), dma((2, H, 2)), dma((H,)), dma((H,)),
             dma((2, H, 2)), dma((2, H, 2)), dma((2, H)), dma((2, H)),
         ],
@@ -437,7 +468,7 @@
         out_shape=(out, out, out),
         in_specs=[anywhere] * 3,
         out_specs=(anywhere,) * 3,
-        scratch_shapes=[dma((3,))],
+        scratch_shapes=[dma((3, chunk))],
         compiler_params=pltpu.CompilerParams(vmem_limit_bytes=4 * 2**20),
         name="results",
     )(*grads)

time: 62.2 us -> 66.1 us (1.063)
  Pallas kernels: 60.7 us -> 64.5 us
    pallas_call x1, Pallas kernels: 59.8 us -> 63.5 us  [body(): pl.pallas_call(functools.partial(main_kernel, H, C), out_shape=(out, out,...]
where the time goes in v4:
time: 66.1 us; the launch traced here: 65.1 us
  Pallas kernels  64.5 us (98%)
    pallas_call x1, Pallas kernels, body(): pl.pallas_call(functools.partial(main_kernel, H, C), out_shape=(out, out,...  63.5 us

profile of v4, /device:TPU:112, one launch (start us, length us, event | category | flops | bytes accessed | tf_op | source)
XLA Modules:
  0.0 65.1 jit_solution(15996978213275191092)
XLA Ops:
  0.6 63.5 %attention.1 = (bf16[2,64,1024]{2,1,0:T(8,128)(2,1)S(1)}, bf16[2,64,1024]{2,1,0:T(8,128)(2,1)S(1)}, bf16[2,64,1024]{2,1,0:T(8,128)(2,1)S(1)}) custom-call(s32[1,256]{1,0:T(1,128)} %bitcast.14, s32[8,256]{1,0:T(8,128)} %bitcast.13, bf16[2,64,1024]{2,1,0:T(8,128)(2,1)} %bitcast.9, bf16[2,64,1024]{2,1,0:T(8,128)(2,1)} %bitcast.10, ...), custom_call_target="tpu_custom_call" | custom-call | tf_op jit(solution)/shard_map/attention/pallas_call | solution.py:440
  64.2 0.9 %results.1 = (bf16[2,64,1024]{2,1,0:T(8,128)(2,1)}, bf16[2,64,1024]{2,1,0:T(8,128)(2,1)}, bf16[2,64,1024]{2,1,0:T(8,128)(2,1)}) custom-call(bf16[2,64,1024]{2,1,0:T(8,128)(2,1)S(1)} %get-tuple-element.9.refs_0_, bf16[2,64,1024]{2,1,0:T(8,128)(2,1)S(1)} %get-tuple-element.10.refs_1_, bf16[2,64,1024]{2,1,0:T(8,128)(2,1)S(1)} %get-tuple-element.11.refs_2_), custom_call_target="tpu_custom_call" | custom-call | tf_op jit(solution)/shard_map/results/pallas_call | solution.py:466

commit v5 on v4

--- a/solution.py
+++ b/solution.py
@@ -33,7 +33,7 @@
 
 
 def main_kernel(heads, ctx_size, slot_in, nbr_in, q_in, k_in, v_in, g_in, dq_out, dk_out, dv_out,
-                slot_ref, nbr_ref, table_vec, table, table_sem,
+                slot_ref, nbr_ref, table_vec, table, table_sem, ring_sem, ctx_sem,
                 q_loc, g_loc, k_span, v_span, run_k, run_v, dq_stage, part_k, part_v, back_k, back_v, sum_k, sum_v,
                 score_buf, weight_buf, mixed_buf, top_buf, total_buf, stat_buf,
                 in_send, in_recv, fwd_send, fwd_recv, dq_send, dq_recv, ret_send, ret_recv, out_send, out_recv):
@@ -68,15 +68,21 @@
     barrier = pltpu.get_barrier_semaphore()
     for d in range(1, H):
         pl.semaphore_signal(barrier, inc=1, device_id={"head": peer(d)}, device_id_type=MESH)
-    for p in ctx_peer:
-        pl.semaphore_signal(barrier, inc=1, device_id={"ctx": p}, device_id_type=MESH)
-    pl.semaphore_wait(barrier, H + 1)
+    @pl.when(h == 0)
+    def _():
+        for p in ctx_peer:
+            pl.semaphore_signal(barrier, inc=1, device_id={"ctx": p}, device_id_type=MESH)
+        pl.semaphore_wait(barrier, H + 1)
+
+    @pl.when(h != 0)
+    def _():
+        pl.semaphore_wait(barrier, H - 1)
 
     order = [0]
     for step in range(1, H):
         order.append(((step + 1) // 2 if step % 2 else H - step // 2) % H)
 
-    incoming = ((k_in, k_span, T), (q_in, q_loc, 0), (v_in, v_span, T), (g_in, g_loc, 0))
+    incoming = ((k_in, k_span, T), (v_in, v_span, T), (q_in, q_loc, 0), (g_in, g_loc, 0))
 
     def in_copy(t, d):
         src, dst, base = incoming[t]
@@ -101,8 +107,17 @@
         for d in order[1:]:
             in_copy(t, d).start()
 
+    @pl.when(h == 0)
+    def _():
+        for way in range(2):
+            pl.semaphore_signal(ring_sem.at[way], inc=1, device_id={"ctx": ctx_peer[way]}, device_id_type=MESH)
+        for way in range(2):
+            pl.semaphore_wait(ring_sem.at[way], 1)
+        for d in range(1, H):
+            pl.semaphore_signal(ctx_sem, inc=1, device_id={"head": peer(d)}, device_id_type=MESH)
+
     def fwd_copy(t, d, way):
-        span = incoming[2 * t][1]
+        span = incoming[t][1]
         chunk = source(d)
         return pltpu.make_async_remote_copy(
             src_ref=span.at[rows(T, chunk)],
@@ -153,16 +168,21 @@
     run_k[pairs] = jnp.zeros(run_k.shape[1:], jnp.float32)
     run_v[pairs] = jnp.zeros(run_v.shape[1:], jnp.float32)
 
-    for d in order:
-        if d == 0:
-            in_own(0).wait()
-        else:
-            in_wait(0, d)
-        for way in range(2):
-            fwd_copy(0, d, way).start()
+    @pl.when(h != 0)
+    def _():
+        pl.semaphore_wait(ctx_sem, 1)
+
+    for t in range(2):
+        for d in order:
+            if d == 0:
+                in_own(t).wait()
+            else:
+                in_wait(t, d)
+            for way in range(2):
+                fwd_copy(t, d, way).start()
 
     def fwd_wait(t, d, way):
-        span = incoming[2 * t][1]
+        span = incoming[t][1]
         chunk = source(d)
         pltpu.make_async_remote_copy(
             src_ref=span.at[rows(T, chunk)],
@@ -297,21 +317,14 @@
 
     turns = H * per_chunk
     in_own(2).wait()
-    for way in range(2):
-        fwd_copy(1, 0, way).start()
-    in_own(1).wait()
     together(Scores(0, 0))
     together(Weights(0, 0), Scores(1, 1))
 
     def first_step(step, carry):
-        d = at_step(step, H)
-        in_wait(1, d)
+        in_wait(2, at_step(step, H))
         turn = step * per_chunk
         together(Weights(turn - 1, 1), Scores(turn, 0))
         together(Weights(turn, 0), Scores(turn + 1, 1))
-        in_wait(2, d)
-        for way in range(2):
-            fwd_copy(1, d, way).start()
         return carry
 
     lax.fori_loop(1, H, first_step, 0)
@@ -445,6 +458,7 @@
         scratch_shapes=[
             pltpu.VMEM((1,) + block_slot.shape, jnp.int32), pltpu.VMEM(neighbours.shape[::-1], jnp.int32),
             pltpu.VMEM((3, NBR, 128), jnp.int32), pltpu.SMEM((3, NBR, 128), jnp.int32), dma((4,)),
+            pltpu.SemaphoreType.REGULAR((2,)), pltpu.SemaphoreType.REGULAR,
             pltpu.VMEM((T, BLOCK_TOK, 128), low), pltpu.VMEM((T, BLOCK_TOK, 128), low),
             pltpu.VMEM((3 * T, BLOCK_TOK, 128), low), pltpu.VMEM((3 * T, BLOCK_TOK, 128), low),
             pltpu.VMEM((pairs + 1, BLOCK_TOK, 128), jnp.float32),

time: 66.1 us -> 61.5 us (0.930)
  Pallas kernels: 64.5 us -> 60.4 us
    pallas_call x1, Pallas kernels: 63.5 us -> 59.5 us  [body(): pl.pallas_call(functools.partial(main_kernel, H, C), out_shape=(out, out,...]
where the time goes in v5:
time: 61.5 us; the launch traced here: 61 us
  Pallas kernels  60.4 us (98%)
  between operations  0.64 us (1%)
    pallas_call x1, Pallas kernels, body(): pl.pallas_call(functools.partial(main_kernel, H, C), out_shape=(out, out,...  59.5 us

profile of v5, /device:TPU:112, one launch (start us, length us, event | category | flops | bytes accessed | tf_op | source)
XLA Modules:
  0.0 61.0 jit_solution(8963000210513518990)
XLA Ops:
  0.6 59.5 %attention.1 = (bf16[2,64,1024]{2,1,0:T(8,128)(2,1)S(1)}, bf16[2,64,1024]{2,1,0:T(8,128)(2,1)S(1)}, bf16[2,64,1024]{2,1,0:T(8,128)(2,1)S(1)}) custom-call(s32[1,256]{1,0:T(1,128)} %bitcast.14, s32[8,256]{1,0:T(8,128)} %bitcast.13, bf16[2,64,1024]{2,1,0:T(8,128)(2,1)} %bitcast.9, bf16[2,64,1024]{2,1,0:T(8,128)(2,1)} %bitcast.10, ...), custom_call_target="tpu_custom_call" | custom-call | tf_op jit(solution)/shard_map/attention/pallas_call | solution.py:453
  60.1 0.9 %results.1 = (bf16[2,64,1024]{2,1,0:T(8,128)(2,1)}, bf16[2,64,1024]{2,1,0:T(8,128)(2,1)}, bf16[2,64,1024]{2,1,0:T(8,128)(2,1)}) custom-call(bf16[2,64,1024]{2,1,0:T(8,128)(2,1)S(1)} %get-tuple-element.9.refs_0_, bf16[2,64,1024]{2,1,0:T(8,128)(2,1)S(1)} %get-tuple-element.10.refs_1_, bf16[2,64,1024]{2,1,0:T(8,128)(2,1)S(1)} %get-tuple-element.11.refs_2_), custom_call_target="tpu_custom_call" | custom-call | tf_op jit(solution)/shard_map/results/pallas_call | solution.py:480

commit v6 on v5

--- a/solution.py
+++ b/solution.py
@@ -317,23 +317,21 @@
 
     turns = H * per_chunk
     in_own(2).wait()
-    together(Scores(0, 0))
-    together(Weights(0, 0), Scores(1, 1))
+    together(*[Scores(k, k) for k in range(per_chunk)])
 
     def first_step(step, carry):
         in_wait(2, at_step(step, H))
         turn = step * per_chunk
-        together(Weights(turn - 1, 1), Scores(turn, 0))
-        together(Weights(turn, 0), Scores(turn + 1, 1))
+        together(*[Weights(turn - per_chunk + k, k) for k in range(per_chunk)],
+                 *[Scores(turn + k, k) for k in range(per_chunk)])
         return carry
 
     lax.fori_loop(1, H, first_step, 0)
-    together(Weights(turns - 1, 1))
+    together(*[Weights(turns - per_chunk + k, k) for k in range(per_chunk)])
 
     span_wait(1)
     in_own(3).wait()
-    together(Mixed(0, 0))
-    together(Gradients(0, 0), Mixed(1, 1))
+    together(*[Mixed(k, k) for k in range(per_chunk)])
 
     def second_step(step, carry):
         in_wait(3, at_step(step, H))
@@ -347,8 +345,8 @@
             dq_copy(at_step(step - 2, H)).start()
 
         turn = step * per_chunk
-        together(Gradients(turn - 1, 1), Mixed(turn, 0))
-        together(Gradients(turn, 0), Mixed(turn + 1, 1))
+        together(*[Gradients(turn - per_chunk + k, k) for k in range(per_chunk)],
+                 *[Mixed(turn + k, k) for k in range(per_chunk)])
         return carry
 
     lax.fori_loop(1, H, second_step, 0)
@@ -356,7 +354,7 @@
         dq_own().start()
     else:
         dq_copy(order[H - 2]).start()
-    together(Gradients(turns - 1, 1))
+    together(*[Gradients(turns - per_chunk + k, k) for k in range(per_chunk)])
     dq_copy(order[H - 1]).start()
 
     back_order = order[::-1]
@@ -467,9 +465,9 @@
             pltpu.VMEM((2 * T, BLOCK_TOK, 128), low), pltpu.VMEM((2 * T, BLOCK_TOK, 128), low),
             pltpu.VMEM((2 * T, BLOCK_TOK, 128), low), pltpu.VMEM((2 * T, BLOCK_TOK, 128), low),
             pltpu.VMEM((T, BLOCK_TOK, 128), low), pltpu.VMEM((T, BLOCK_TOK, 128), low),
-            pltpu.VMEM((2, NBR * BLOCK_TOK, 128), jnp.float32), pltpu.VMEM((T, NBR * BLOCK_TOK, 128), jnp.float32),
-            pltpu.VMEM((2, NBR * BLOCK_TOK, 128), jnp.float32),
-            *[pltpu.VMEM((n, 8, 128), jnp.float32) for n in (2, T, 2)],
+            pltpu.VMEM((chunk, NBR * BLOCK_TOK, 128), jnp.float32), pltpu.VMEM((T, NBR * BLOCK_TOK, 128), jnp.float32),
+            pltpu.VMEM((chunk, NBR * BLOCK_TOK, 128), jnp.float32),
+            *[pltpu.VMEM((n, 8, 128), jnp.float32) for n in (chunk, T, chunk)],
             dma((4, H)), dma((4, H)), dma((2, H, 2)), dma((2, H, 2)), dma((H,)), dma((H,)),
             dma((2, H, 2)), dma((2, H, 2)), dma((2, H)), dma((2, H)),
         ],

time: 61.5 us -> 61.4 us (level)
  no operation moved by 1% of the time
where the time goes in v6:
time: 61.4 us; the launch traced here: 60.9 us
  Pallas kernels  60.2 us (98%)
  between operations  0.64 us (1%)
    pallas_call x1, Pallas kernels, body(): pl.pallas_call(functools.partial(main_kernel, H, C), out_shape=(out, out,...  59.3 us

profile of v6, /device:TPU:112, one launch (start us, length us, event | category | flops | bytes accessed | tf_op | source)
XLA Modules:
  0.0 60.9 jit_solution(9364051045115130709)
XLA Ops:
  0.6 59.3 %attention.1 = (bf16[2,64,1024]{2,1,0:T(8,128)(2,1)S(1)}, bf16[2,64,1024]{2,1,0:T(8,128)(2,1)S(1)}, bf16[2,64,1024]{2,1,0:T(8,128)(2,1)S(1)}) custom-call(s32[1,256]{1,0:T(1,128)} %bitcast.14, s32[8,256]{1,0:T(8,128)} %bitcast.13, bf16[2,64,1024]{2,1,0:T(8,128)(2,1)} %bitcast.9, bf16[2,64,1024]{2,1,0:T(8,128)(2,1)} %bitcast.10, ...), custom_call_target="tpu_custom_call" | custom-call | tf_op jit(solution)/shard_map/attention/pallas_call | solution.py:451
  60.0 0.9 %results.1 = (bf16[2,64,1024]{2,1,0:T(8,128)(2,1)}, bf16[2,64,1024]{2,1,0:T(8,128)(2,1)}, bf16[2,64,1024]{2,1,0:T(8,128)(2,1)}) custom-call(bf16[2,64,1024]{2,1,0:T(8,128)(2,1)S(1)} %get-tuple-element.9.refs_0_, bf16[2,64,1024]{2,1,0:T(8,128)(2,1)S(1)} %get-tuple-element.10.refs_1_, bf16[2,64,1024]{2,1,0:T(8,128)(2,1)S(1)} %get-tuple-element.11.refs_2_), custom_call_target="tpu_custom_call" | custom-call | tf_op jit(solution)/shard_map/results/pallas_call | solution.py:478

commit v7 on v6

--- a/solution.py
+++ b/solution.py
@@ -102,9 +102,10 @@
             send_sem=in_send.at[t, d], recv_sem=in_recv.at[t, d],
             device_id={"head": peer(d)}, device_id_type=MESH).wait_recv()
 
+    far_first = order[:0:-1]
     for t in range(4):
         in_own(t).start()
-        for d in order[1:]:
+        for d in far_first if t < 2 else order[1:]:
             in_copy(t, d).start()
 
     @pl.when(h == 0)
@@ -173,7 +174,7 @@
         pl.semaphore_wait(ctx_sem, 1)
 
     for t in range(2):
-        for d in order:
+        for d in order[:1] + far_first:
             if d == 0:
                 in_own(t).wait()
             else:

time: 61.4 us -> 61.8 us (level)
  no operation moved by 1% of the time
where the time goes in v7:
time: 61.8 us; the launch traced here: 61.2 us
  Pallas kernels  60.5 us (98%)
  between operations  0.64 us (1%)
    pallas_call x1, Pallas kernels, body(): pl.pallas_call(functools.partial(main_kernel, H, C), out_shape=(out, out,...  59.6 us

profile of v7, /device:TPU:112, one launch (start us, length us, event | category | flops | bytes accessed | tf_op | source)
XLA Modules:
  0.0 61.2 jit_solution(184197368692159802)
XLA Ops:
  0.6 59.6 %attention.1 = (bf16[2,64,1024]{2,1,0:T(8,128)(2,1)S(1)}, bf16[2,64,1024]{2,1,0:T(8,128)(2,1)S(1)}, bf16[2,64,1024]{2,1,0:T(8,128)(2,1)S(1)}) custom-call(s32[1,256]{1,0:T(1,128)} %bitcast.14, s32[8,256]{1,0:T(8,128)} %bitcast.13, bf16[2,64,1024]{2,1,0:T(8,128)(2,1)} %bitcast.9, bf16[2,64,1024]{2,1,0:T(8,128)(2,1)} %bitcast.10, ...), custom_call_target="tpu_custom_call" | custom-call | tf_op jit(solution)/shard_map/attention/pallas_call | solution.py:452
  60.2 0.9 %results.1 = (bf16[2,64,1024]{2,1,0:T(8,128)(2,1)}, bf16[2,64,1024]{2,1,0:T(8,128)(2,1)}, bf16[2,64,1024]{2,1,0:T(8,128)(2,1)}) custom-call(bf16[2,64,1024]{2,1,0:T(8,128)(2,1)S(1)} %get-tuple-element.9.refs_0_, bf16[2,64,1024]{2,1,0:T(8,128)(2,1)S(1)} %get-tuple-element.10.refs_1_, bf16[2,64,1024]{2,1,0:T(8,128)(2,1)S(1)} %get-tuple-element.11.refs_2_), custom_call_target="tpu_custom_call" | custom-call | tf_op jit(solution)/shard_map/results/pallas_call | solution.py:479

commit v8 on v6

--- a/solution.py
+++ b/solution.py
@@ -115,6 +115,13 @@
             pl.semaphore_wait(ring_sem.at[way], 1)
         for d in range(1, H):
             pl.semaphore_signal(ctx_sem, inc=1, device_id={"head": peer(d)}, device_id_type=MESH)
+
+    def crossing_first(start):
+        for first in range(2):
+            @pl.when(lax.rem(c, 2) == first)
+            def _():
+                start(first)
+                start(1 - first)
 
     def fwd_copy(t, d, way):
         span = incoming[t][1]
@@ -178,8 +185,7 @@
                 in_own(t).wait()
             else:
                 in_wait(t, d)
-            for way in range(2):
-                fwd_copy(t, d, way).start()
+            crossing_first(lambda way: fwd_copy(t, d, way).start())
 
     def fwd_wait(t, d, way):
         span = incoming[t][1]
@@ -377,9 +383,7 @@
                 end = table[2, 0, region * per_ctx + block]
                 part_k[way * T + block] = (run_k[end] * scale).astype(jnp.bfloat16)
                 part_v[way * T + block] = run_v[end].astype(jnp.bfloat16)
-        for way in range(2):
-            for which in range(2):
-                ret_copy(d, way, which).start()
+        crossing_first(lambda way: [ret_copy(d, way, which).start() for which in range(2)])
 
     def out_copy(d, which):
         chunk = peer(d)

time: 61.4 us -> 61.4 us (level)
  no operation moved by 1% of the time
where the time goes in v8:
time: 61.4 us; the launch traced here: 60.9 us
  Pallas kernels  60.3 us (98%)
  between operations  0.64 us (1%)
    pallas_call x1, Pallas kernels, body(): pl.pallas_call(functools.partial(main_kernel, H, C), out_shape=(out, out,...  59.3 us

profile of v8, /device:TPU:112, one launch (start us, length us, event | category | flops | bytes accessed | tf_op | source)
XLA Modules:
  0.0 60.9 jit_solution(14583550316087995014)
XLA Ops:
  0.6 59.3 %attention.1 = (bf16[2,64,1024]{2,1,0:T(8,128)(2,1)S(1)}, bf16[2,64,1024]{2,1,0:T(8,128)(2,1)S(1)}, bf16[2,64,1024]{2,1,0:T(8,128)(2,1)S(1)}) custom-call(s32[1,256]{1,0:T(1,128)} %bitcast.14, s32[8,256]{1,0:T(8,128)} %bitcast.13, bf16[2,64,1024]{2,1,0:T(8,128)(2,1)} %bitcast.9, bf16[2,64,1024]{2,1,0:T(8,128)(2,1)} %bitcast.10, ...), custom_call_target="tpu_custom_call" | custom-call | tf_op jit(solution)/shard_map/attention/pallas_call | solution.py:455
  60.0 0.9 %results.1 = (bf16[2,64,1024]{2,1,0:T(8,128)(2,1)}, bf16[2,64,1024]{2,1,0:T(8,128)(2,1)}, bf16[2,64,1024]{2,1,0:T(8,128)(2,1)}) custom-call(bf16[2,64,1024]{2,1,0:T(8,128)(2,1)S(1)} %get-tuple-element.9.refs_0_, bf16[2,64,1024]{2,1,0:T(8,128)(2,1)S(1)} %get-tuple-element.10.refs_1_, bf16[2,64,1024]{2,1,0:T(8,128)(2,1)S(1)} %get-tuple-element.11.refs_2_), custom_call_target="tpu_custom_call" | custom-call | tf_op jit(solution)/shard_map/results/pallas_call | solution.py:482
